TPU v7x, 128 devices: a whole 4x4x4 slice. The times are simulated.
128 devices in a mesh: mem: 16 (over z, x), sub: 8 (over y, core).
Axes of the slice: x: 4, y: 4, z: 4, core: 2. Of those that a mesh axis runs over, the one named last changes fastest.
Arguments:
- ensemble: float32 [64, 3, 256, 2048], P('mem', None, 'sub'), may hold values from -6 to 6
- sea_depth: float32 [256, 2048], P('sub'), may hold values from 0.5 to 2
- cutoff: int32 [256, 2048], P('sub', 'mem'), may hold values from 16 to 64
- obs_index: int32 [4, 256], replicated, may hold values from 0 to 524287
- obs_value: float32 [4, 256], replicated, may hold values from -6 to 6
- obs_var: float32 [4, 256], replicated, may hold values from 0.5 to 2
Outputs:
- analysis: float32 [64, 3, 256, 2048], P(None, None, 'sub', 'mem')
All inputs are finite; a program needn't handle non-finite values.
Results may differ from a plain program's by a relative error of at most 0.0001.
Values sent between devices are 32-bit elements; how exact they have to be, the bound alone decides.
A program may use at most 192 MiB of HBM per device.

v0:
```python
import jax
import jax.numpy as jnp
from jax import lax
from jax.sharding import PartitionSpec as P

STEPS = 4
BATCHES = 4


step_size = 0.3
coriolis = 0.2
highest = lax.Precision.HIGHEST


def padded(shard, sides, width):
    for axis, dim in sides:
        peers, length = (lax.axis_size(axis), shard.shape[dim])
        up = [(i, (i + 1) % peers) for i in range(peers)]
        down = [(j, i) for i, j in up]
        last = lax.slice_in_dim(shard, length - width, length, axis=dim)
        leading = lax.slice_in_dim(shard, 0, width, axis=dim)
        before = lax.ppermute(last, axis, up)
        after = lax.ppermute(leading, axis, down)
        shard = jnp.concatenate([before, shard, after], axis=dim)
    return shard


def across_cols(field):
    return (jnp.roll(field, -1, 2) - jnp.roll(field, 1, 2)) * 0.5


def momentum(height, east_wind, north_wind):
    height_ext = padded(height, (("sub", 1),), 1)
    height_dx = (height_ext[:, 2:] - height_ext[:, :-2]) * 0.5
    east_new = east_wind + step_size * (coriolis * north_wind - height_dx)
    north_new = north_wind + step_size * (-coriolis * east_wind - across_cols(height))
    return (east_new, north_new)


def continuity(height, east_wind, north_wind, sea_depth):
    flux_ext = padded(sea_depth * east_wind, (("sub", 1),), 1)
    divergence = (flux_ext[:, 2:] - flux_ext[:, :-2]) * 0.5 + across_cols(sea_depth * north_wind)
    return height - step_size * divergence


def localize(obs_x, obs_y, cell_x, cell_y, radius_sq, size_x, size_y):
    gap_x = jnp.abs(cell_x[None, :] - obs_x[:, None])
    gap_x = jnp.minimum(gap_x, size_x - gap_x)
    gap_y = jnp.abs(cell_y[None, :] - obs_y[:, None])
    gap_y = jnp.minimum(gap_y, size_y - gap_y)
    dist_sq = (gap_x * gap_x + gap_y * gap_y).astype(jnp.float32)
    dist_ratio = dist_sq / radius_sq[None, :]
    return jnp.square(jnp.maximum(1.0 - dist_ratio, 0.0))


def analysis_weights(prior_obs, values, variance):
    member_count = prior_obs.shape[1]
    obs_mean = jnp.mean(prior_obs, 1)
    obs_anom = prior_obs - obs_mean[:, None]
    innov_cov = jnp.dot(obs_anom, obs_anom.T, precision=highest) / (member_count - 1) + jnp.diag(
        variance
    )
    factor = jnp.linalg.cholesky(innov_cov)
    right_side = jnp.concatenate([(values - obs_mean)[:, None], obs_anom], 1)
    solved = jax.scipy.linalg.cho_solve((factor, True), right_side)
    return (obs_anom, solved[:, :1] - 0.5 * solved[:, 1:])


def update_state(members, obs_anom, weights_mix, loc_weight, cell_count):
    member_count = members.shape[0]
    obs_count = obs_anom.shape[0]
    state_anom = members - jnp.mean(members, 0)
    cross_cov = jnp.dot(obs_anom, state_anom, precision=highest) / (member_count - 1)
    loc_gain = (cross_cov.reshape(obs_count, 3, cell_count) * loc_weight[:, None, :]).reshape(
        obs_count, 3 * cell_count
    )
    return members + jnp.dot(weights_mix.T, loc_gain, precision=highest)


def local(ensemble, sea_depth, cutoff, obs_index, obs_value, obs_var):
    height = ensemble[:, 0]
    east_wind = ensemble[:, 1]
    north_wind = ensemble[:, 2]
    for step_id in range(STEPS - 1):
        east_wind, north_wind = momentum(height, east_wind, north_wind)
        height = continuity(height, east_wind, north_wind, sea_depth)
    east_wind, north_wind = momentum(height, east_wind, north_wind)
    height = continuity(height, east_wind, north_wind, sea_depth)
    point_state = lax.all_to_all(
        jnp.stack([height, east_wind, north_wind], 1),
        "mem",
        split_axis=3,
        concat_axis=0,
        tiled=True,
    )
    member_count = point_state.shape[0]
    row_count, col_block = cutoff.shape
    x_start = lax.axis_index("sub") * row_count
    y_start = lax.axis_index("mem") * col_block
    size_x = row_count * lax.axis_size("sub")
    size_y = col_block * lax.axis_size("mem")
    cell_count = row_count * col_block
    cell_ids = jnp.arange(cell_count, dtype=jnp.int32)
    cell_x = x_start + cell_ids // col_block
    cell_y = y_start + cell_ids % col_block
    radius_sq = jnp.square(cutoff.reshape(cell_count).astype(jnp.float32))
    members = point_state.reshape(member_count, 3 * cell_count)
    for batch_id in range(BATCHES):
        obs_cell = obs_index[batch_id]
        obs_x = obs_cell // size_y
        obs_y = obs_cell % size_y
        select_obs_x = obs_cell // size_y
        select_obs_y = obs_cell % size_y
        inside = (
            (select_obs_x >= x_start)
            & (select_obs_x < x_start + row_count)
            & (select_obs_y >= y_start)
            & (select_obs_y < y_start + col_block)
        )
        local_id = (select_obs_x - x_start) * col_block + (select_obs_y - y_start)
        local_part = lax.dot_general(
            ((local_id[:, None] == cell_ids[None, :]) & inside[:, None]).astype(jnp.float32),
            members[:, :cell_count],
            (((1,), (1,)), ((), ())),
            precision=highest,
        )
        prior_obs = lax.psum(local_part, ("mem", "sub"))
        obs_anom, weights_mix = analysis_weights(prior_obs, obs_value[batch_id], obs_var[batch_id])
        loc_weight = localize(obs_x, obs_y, cell_x, cell_y, radius_sq, size_x, size_y)
        members = update_state(members, obs_anom, weights_mix, loc_weight, cell_count)
    return members.reshape(member_count, 3, row_count, col_block)


def solution(mesh):
    return jax.shard_map(
        local,
        mesh=mesh,
        in_specs=(P("mem", None, "sub", None), P("sub", None), P("sub", "mem"), P(), P(), P()),
        out_specs=P(None, None, "sub", "mem"),
        check_vma=False,
    )
```

profile of v0, /device:TPU:1, one launch (start us, length us, event | category | flops | bytes accessed | tf_op | source)
XLA Modules:
  0.0 1229.5 jit_solution(545508524932749431)
XLA Ops:
  83.5 15.4 %reshape.856 = f32[16,1,49152]{2,1,0:T(1,128)} reshape(f32[2048,3,4,32]{3,2,1,0:T(4,128)} %bitcast.231) | data formatting | bytes 6291456
  106.8 14.0 %fusion.34 = (f32[256,4096]{0,1:T(8,128)}, f32[256,4096]{0,1:T(8,128)}, f32[256,4096]{0,1:T(8,128)}, f32[256,4096]{0,1:T(8,128)S(1)}) fusion(s32[256]{0:T(256)S(1)} %copy-done.18, s32[256]{0:T(256)S(1)} %copy-done.17, f32[4096]{0:T(1024)S(1)} %multiply_bitcast_fusion, s32[4096]{0:T(1024)S(1)} %copy-done.16, s32[4096]{0:T(1024)S(1)} %copy-done.15, ...), kind=kLoop, calls=%fused_computation.58 | loop fusion | flops 67108864 | bytes 16834560 | tf_op jit(solution)/shard_map/square | solution.py:53
  126.4 12.6 %copy.123 = f32[256,12288]{1,0:T(8,128)} copy(f32[256,12288]{0,1:T(8,128)} %bitcast.227) | data formatting | bytes 25165824 | tf_op jit(solution)/shard_map/mul | solution.py:74
  146.8 12.6 %copy.126 = f32[256,12288]{1,0:T(8,128)} copy(f32[256,12288]{0,1:T(8,128)} %bitcast.228) | data formatting | bytes 25165824 | tf_op jit(solution)/shard_map/mul | solution.py:74
  167.2 12.6 %copy.129 = f32[256,12288]{1,0:T(8,128)} copy(f32[256,12288]{0,1:T(8,128)} %bitcast.229) | data formatting | bytes 25165824 | tf_op jit(solution)/shard_map/mul | solution.py:74
  187.5 12.8 %copy.132 = f32[256,12288]{1,0:T(8,128)} copy(f32[256,12288]{0,1:T(8,128)} %bitcast.230) | data formatting | bytes 25165824 | tf_op jit(solution)/shard_map/mul | solution.py:74
  203.2 10.8 reduce.9
  214.1 15.0 %reshape.857 = f32[2048,3,4,32]{3,2,1,0:T(4,128)} reshape(f32[16,49152]{1,0:T(8,128)} %reduce.9) | data formatting | bytes 6291456
  247.5 141.1 %all-reduce.6.cloned.1.call-done = f32[256,64]{0,1:T(8,128)} async-done(((f32[256,64]{0,1:T(8,128)}), f32[256,64]{0,1:T(8,128)}) %all-reduce.6.cloned.1.call-update) | async-done | bytes 65552 | tf_op jit(solution)/shard_map/psum | solution.py:127
  393.3 11.7 cholesky.214
  406.2 10.6 custom-call.19
  419.7 12.5 %cholesky.231 = f32[128,128]{1,0:T(8,128)S(1)} custom-call(f32[128,128]{1,0:T(8,128)} %convolution_subtract_fusion.3), custom_call_target="Cholesky" | custom-call | tf_op jit(solution)/shard_map/jit(cholesky)/cholesky | solution.py:63
  442.7 21.1 %custom-call.20 = f32[2,128,128]{1,2,0:T(8,128)} custom-call(f32[2,128,128]{2,1,0:T(8,128)} %get-tuple-element.33), custom_call_target="InvertDiagBlocksLowerTriangular" | custom-call | tf_op jit(solution)/shard_map/jit(_cho_solve)/triangular_solve | solution.py:65
  469.3 13.6 %fusion.3 = f32[256,12288]{1,0:T(8,128)S(1)} fusion(f32[256,12288]{1,0:T(8,128)} %copy.123, f32[256,64]{0,1:T(8,128)S(1)} %broadcast_subtract_fusion.3, f32[64,12288]{1,0:T(8,128)S(1)} %reshape.826, f32[12288]{0:T(1024)} %bitcast.240), kind=kOutput, calls=%fused_computation.15 | convolution fusion | flops 2422996992 | bytes 28426240 | tf_op jit(solution)/shard_map/dot_general | solution.py:73
  496.6 135.9 %all-reduce.8.cloned.1.call-done = f32[256,64]{0,1:T(8,128)} async-done(((f32[256,64]{0,1:T(8,128)}), f32[256,64]{0,1:T(8,128)}) %all-reduce.8.cloned.1.call-update) | async-done | bytes 65552 | tf_op jit(solution)/shard_map/psum | solution.py:127
  637.2 11.7 cholesky.248
  649.6 10.6 custom-call.21
  663.0 12.5 %cholesky.265 = f32[128,128]{1,0:T(8,128)S(1)} custom-call(f32[128,128]{1,0:T(8,128)} %convolution_subtract_fusion.2), custom_call_target="Cholesky" | custom-call | tf_op jit(solution)/shard_map/jit(cholesky)/cholesky | solution.py:63
  686.1 21.1 %custom-call.22 = f32[2,128,128]{1,2,0:T(8,128)} custom-call(f32[2,128,128]{2,1,0:T(8,128)} %get-tuple-element.34), custom_call_target="InvertDiagBlocksLowerTriangular" | custom-call | tf_op jit(solution)/shard_map/jit(_cho_solve)/triangular_solve | solution.py:65
  712.7 13.6 %fusion.2 = f32[256,12288]{1,0:T(8,128)S(1)} fusion(f32[256,12288]{1,0:T(8,128)} %copy.126, f32[256,64]{0,1:T(8,128)S(1)} %broadcast_subtract_fusion.2, f32[64,12288]{1,0:T(8,128)S(1)} %get-tuple-element.195, f32[12288]{0:T(1024)} %broadcast_multiply_fusion.10), kind=kOutput, calls=%fused_computation.13 | convolution fusion | flops 2422996992 | bytes 28426240 | tf_op jit(solution)/shard_map/dot_general | solution.py:73
  740.1 135.9 %all-reduce.10.cloned.1.call-done = f32[256,64]{0,1:T(8,128)} async-done(((f32[256,64]{0,1:T(8,128)}), f32[256,64]{0,1:T(8,128)}) %all-reduce.10.cloned.1.call-update) | async-done | bytes 65552 | tf_op jit(solution)/shard_map/psum | solution.py:127
  880.7 11.7 cholesky.282
  893.1 10.6 custom-call.23
  906.5 12.5 %cholesky.299 = f32[128,128]{1,0:T(8,128)S(1)} custom-call(f32[128,128]{1,0:T(8,128)} %convolution_subtract_fusion.1), custom_call_target="Cholesky" | custom-call | tf_op jit(solution)/shard_map/jit(cholesky)/cholesky | solution.py:63
  929.9 21.1 %custom-call.24 = f32[2,128,128]{1,2,0:T(8,128)} custom-call(f32[2,128,128]{2,1,0:T(8,128)} %get-tuple-element.35), custom_call_target="InvertDiagBlocksLowerTriangular" | custom-call | tf_op jit(solution)/shard_map/jit(_cho_solve)/triangular_solve | solution.py:65
  955.9 13.6 %fusion.1 = f32[256,12288]{1,0:T(8,128)S(1)} fusion(f32[256,12288]{1,0:T(8,128)} %copy.129, f32[256,64]{0,1:T(8,128)S(1)} %broadcast_subtract_fusion.1, f32[64,12288]{1,0:T(8,128)S(1)} %copy-done.1, f32[12288]{0:T(1024)} %broadcast_multiply_fusion.9), kind=kOutput, calls=%fused_computation.11 | convolution fusion | flops 2422996992 | bytes 28426240 | tf_op jit(solution)/shard_map/dot_general | solution.py:73
  982.9 136.2 %all-reduce.12.cloned.1.call-done = f32[256,64]{0,1:T(8,128)} async-done(((f32[256,64]{0,1:T(8,128)}), f32[256,64]{0,1:T(8,128)}) %all-reduce.12.cloned.1.call-update) | async-done | bytes 65552 | tf_op jit(solution)/shard_map/psum | solution.py:127
  1123.8 11.8 cholesky.316
  1136.3 10.6 custom-call.25
  1149.8 12.5 %cholesky.333 = f32[128,128]{1,0:T(8,128)S(1)} custom-call(f32[128,128]{1,0:T(8,128)} %convolution_subtract_fusion), custom_call_target="Cholesky" | custom-call | tf_op jit(solution)/shard_map/jit(cholesky)/cholesky | solution.py:63
  1173.2 21.1 %custom-call.26 = f32[2,128,128]{1,2,0:T(8,128)} custom-call(f32[2,128,128]{2,1,0:T(8,128)} %get-tuple-element.36), custom_call_target="InvertDiagBlocksLowerTriangular" | custom-call | tf_op jit(solution)/shard_map/jit(_cho_solve)/triangular_solve | solution.py:65
  1199.1 13.4 %fusion = f32[256,12288]{1,0:T(8,128)S(1)} fusion(f32[256,12288]{1,0:T(8,128)} %copy.132, f32[256,64]{0,1:T(8,128)S(1)} %broadcast_subtract_fusion, f32[64,12288]{1,0:T(8,128)S(1)} %copy-done.5, f32[12288]{0:T(1024)} %broadcast_multiply_fusion.8), kind=kOutput, calls=%fused_computation.9 | convolution fusion | flops 2422996992 | bytes 28426240 | tf_op jit(solution)/shard_map/dot_general | solution.py:73
  (307 shorter events, 301.1 us)
Async XLA Ops:
  10.9 7.9 collective-permute-start
  12.3 6.5 collective-permute-start.1
  24.7 3.4 collective-permute-start.2
  26.0 3.7 collective-permute-start.3
  31.8 4.7 collective-permute-start.4
  35.6 1.2 collective-permute-start.5
  40.0 4.2 collective-permute-start.6
  43.4 1.2 collective-permute-start.7
  46.3 4.2 collective-permute-start.8
  49.7 1.2 collective-permute-start.9
  54.2 4.2 collective-permute-start.10
  57.5 1.2 collective-permute-start.11
  60.5 4.2 collective-permute-start.12
  63.8 1.2 collective-permute-start.13
  68.2 4.2 collective-permute-start.14
  71.6 1.2 collective-permute-start.15
  99.0 103.7 %all-to-all-start = ((f32[16,1,49152]{2,1,0:T(1,128)}), f32[16,1,49152]{2,1,0:T(1,128)S(1)}, u32[]{:S(2)}, u32[]{:S(2)}) async-start(f32[16,1,49152]{2,1,0:T(1,128)} %reshape.856), calls=%async_computation | async-start | bytes 6291456 | tf_op jit(solution)/shard_map/all_to_all | solution.py:89
  106.6 282.0 %all-reduce.6.cloned.1.call-start = ((), (), s32[]{:S(2)}) async-start(), calls=%async_computation.1 | async-start | bytes 131072 | tf_op jit(solution)/shard_map/psum | solution.py:127
  187.5 15.1 %copy-start.27 = (f32[4,256]{1,0:T(4,128)S(1)}, f32[4,256]{1,0:T(4,128)}, u32[]{:S(2)}) copy-start(f32[4,256]{1,0:T(4,128)} %param.14) | copy-start | bytes 12292
  243.5 225.8 %copy-start.2 = (f32[64,12288]{1,0:T(8,128)}, f32[64,12288]{1,0:T(8,128)S(1)}, u32[]{:S(2)}) copy-start(f32[64,12288]{1,0:T(8,128)S(1)} %reshape.826) | copy-start | bytes 9437188
  246.7 385.8 %all-reduce.8.cloned.1.call-start = ((), (), s32[]{:S(2)}) async-start(), calls=%async_computation.2 | async-start | bytes 131072 | tf_op jit(solution)/shard_map/psum | solution.py:127
  442.7 40.3 %copy-start.35 = (s32[2,2]{1,0:T(2,128)}, s32[2,2]{1,0:T(2,128)S(1)}, u32[]{:S(2)}) copy-start(s32[2,2]{1,0:T(2,128)S(1)} %get-tuple-element.440) | copy-start | bytes 52
  483.0 9.6 copy-start.30
  495.7 380.3 %all-reduce.10.cloned.1.call-start = ((), (), s32[]{:S(2)}) async-start(), calls=%async_computation.3 | async-start | bytes 131072 | tf_op jit(solution)/shard_map/psum | solution.py:127
  726.4 9.7 copy-start.29
  726.4 9.7 copy-start.32
  734.4 216.7 %copy-start.25 = (f32[4,256]{1,0:T(4,128)S(1)}, f32[4,256]{1,0:T(4,128)}, u32[]{:S(2)}) copy-start(f32[4,256]{1,0:T(4,128)} %param.13) | copy-start | bytes 12292
  739.2 216.7 %copy-start.1 = (f32[64,12288]{1,0:T(8,128)S(1)}, f32[64,12288]{1,0:T(8,128)}, u32[]{:S(2)}) copy-start(f32[64,12288]{1,0:T(8,128)} %copy-done) | copy-start | bytes 9437188
  739.2 379.9 %all-reduce.12.cloned.1.call-start = ((), (), s32[]{:S(2)}) async-start(), calls=%async_computation.4 | async-start | bytes 131072 | tf_op jit(solution)/shard_map/psum | solution.py:127
  969.5 9.7 copy-start.28
  969.5 9.7 copy-start.31
  982.3 216.8 %copy-start.5 = (f32[64,12288]{1,0:T(8,128)S(1)}, f32[64,12288]{1,0:T(8,128)}, u32[]{:S(2)}) copy-start(f32[64,12288]{1,0:T(8,128)} %copy-done.4) | copy-start | bytes 9437188
  (25 other events, 125.0 us)
Sparse Core Ops, SparseCore 0:
  246.8 141.7 all-reduce.5
  495.8 136.6 all-reduce.7
  739.3 136.6 all-reduce.9
  982.4 136.6 all-reduce.11
where the time goes:
time: 1240 us; the launch traced here: 1230 us
  waiting for transfers between devices  559 us (45%)
  other arithmetic  300 us (24%)
  local copies, waits for them, and re-layouts  185 us (15%)
  matrix products  132 us (11%)
  starting transfers between devices  33.5 us (3%)
  between operations  19.3 us (2%)
    psum x4, waiting for transfers between devices, local(): prior_obs = lax.psum(local_part, ('mem', 'sub'))  549 us
    another operation x27, other arithmetic, analysis_weights(): factor = jnp.linalg.cholesky(innov_cov)  148 us
    another operation x9, other arithmetic, analysis_weights(): solved = jax.scipy.linalg.cho_solve((factor, True), right_side)  88.9 us
    mul x8, local copies, waits for them, and re-layouts, update_state(): cross_cov.reshape(obs_count, 3, cell_count) * loc_weight[:, None, :]  79.6 us
    dot_general x4, matrix products, update_state(): jnp.dot(obs_anom, state_anom, precision=highest) / (member_count - 1)  54.3 us
    unnamed x76, local copies, waits for them, and re-layouts  41 us
    dot_general x4, matrix products, update_state(): return members + jnp.dot(weights_mix.T, loc_gain, precision=highest)  33.4 us
    another operation x29, local copies, waits for them, and re-layouts, analysis_weights(): solved = jax.scipy.linalg.cho_solve((factor, True), right_side)  27.8 us
  transfers between devices with their start and end apart: 21, of which 18 were waited for; matrix products, arithmetic and copies ran while one was open for 8% of the time, Pallas kernels for 0%

commit v1 on v0

v1 whole, which is shorter than its diff:
```python
import functools

import jax
import jax.numpy as jnp
from jax import lax
from jax.experimental import pallas as pl
from jax.experimental.pallas import tpu as pltpu
from jax.sharding import PartitionSpec as P

STEPS = 4
BATCHES = 4
DT = 0.3
CORIOLIS = 0.2
MESH = pl.DeviceIdType.MESH
HIGHEST = lax.Precision.HIGHEST
F32 = jnp.float32
BF16 = jnp.bfloat16
HALO = 8
CHUNK = 32
LANES = 128


def nt(a, b, precision=None):
    return lax.dot_general(
        a, b, (((1,), (1,)), ((), ())), precision=precision, preferred_element_type=F32
    )


def nn(a, b, precision=None):
    return lax.dot_general(
        a, b, (((1,), (0,)), ((), ())), precision=precision, preferred_element_type=F32
    )


def split2(x):
    hi = x.astype(BF16)
    return hi, (x - hi.astype(F32)).astype(BF16)


def iota(shape, dim):
    return lax.broadcasted_iota(jnp.int32, shape, dim)


def forecast_kernel(
    ens_ref, depth_ref, cut_ref, obs_ref,
    out_ref, prior_ref,
    ext, dep, gbuf, part, slots, mine,
    lsem, hs_sem, hr_sem, ds_sem, dr_sem, s1_sem, r1_sem, s2_sem, r2_sem,
):
    members, fields, rows, cols = ens_ref.shape
    tiles = cols // LANES
    me = lax.axis_index("mem")
    sub = lax.axis_index("sub")
    n_mem = lax.axis_size("mem")
    n_sub = lax.axis_size("sub")
    nobs = obs_ref.shape[1]

    barrier = pltpu.get_barrier_semaphore()
    for k in range(1, n_sub):
        pl.semaphore_signal(barrier, inc=1, device_id=(me, lax.rem(sub + k, n_sub)), device_id_type=MESH)
    for k in range(1, n_mem):
        pl.semaphore_signal(barrier, inc=1, device_id=(lax.rem(me + k, n_mem), sub), device_id_type=MESH)

    local = []
    cp = pltpu.make_async_copy(depth_ref, dep.at[pl.ds(HALO, rows)], lsem.at[members])
    cp.start()
    local.append(cp)
    for m in range(members):
        cp = pltpu.make_async_copy(ens_ref.at[m], ext.at[m, :, pl.ds(HALO, rows)], lsem.at[m])
        cp.start()
        local.append(cp)
    pl.semaphore_wait(barrier, n_sub - 1 + n_mem - 1)

    up = lax.rem(sub + n_sub - 1, n_sub)
    down = lax.rem(sub + 1, n_sub)
    halo = []
    for d, (peer, src, dst) in enumerate(((up, 0, HALO + rows), (down, rows - HALO, 0))):
        cp = pltpu.make_async_remote_copy(
            depth_ref.at[pl.ds(src, HALO)], dep.at[pl.ds(dst, HALO)],
            ds_sem.at[d], dr_sem.at[d], device_id=(me, peer), device_id_type=MESH)
        cp.start()
        halo.append(cp)
    for m in range(members):
        for d, (peer, src, dst) in enumerate(((up, 0, HALO + rows), (down, rows - HALO, 0))):
            cp = pltpu.make_async_remote_copy(
                ens_ref.at[m, :, pl.ds(src, HALO)], ext.at[m, :, pl.ds(dst, HALO)],
                hs_sem.at[d, m], hr_sem.at[d, m], device_id=(me, peer), device_id_type=MESH)
            cp.start()
            halo.append(cp)

    obs_x = obs_ref[0:1, :]
    obs_y = obs_ref[1:2, :]
    local_x = obs_x - sub * rows
    in_rows = (local_x >= 0) & (local_x < rows)
    combo = jnp.where(in_rows, (obs_y // LANES) * rows + local_x, -1)
    lane_of = obs_y % LANES

    in_block = in_rows & (obs_y // LANES == me)
    pick_row = jnp.where(in_block, local_x, -1)
    cut_t = jnp.transpose(cut_ref[...].astype(F32))
    row_hot = jnp.where(iota((rows, nobs), 0) == pick_row, 1.0, 0.0)
    cut_cols = nn(cut_t.astype(BF16), row_hot.astype(BF16))
    cut_obs = jnp.sum(jnp.where(iota((LANES, nobs), 0) == lane_of, cut_cols, 0.0), 0, keepdims=True)
    for q in range(nobs // LANES):
        mine[pl.ds(members * 8 + q, 1), :] = cut_obs[:, q * LANES:(q + 1) * LANES]

    halo[0].wait()
    halo[1].wait()
    for cp in local:
        cp.wait()
    for cp in halo[2:]:
        cp.wait()

    height = rows + 2 * HALO
    lane = iota((height, LANES), 1)

    def cols_of(t):
        return pl.ds(t * LANES, LANES)

    def member_body(m, _):
        def step_body(s, carry):
            def h_tile(t):
                return ext[m, 0, :, cols_of(t)]

            def g_tile(t):
                return gbuf[:, cols_of(t)]

            for t in range(tiles):
                h = h_tile(t)
                nxt = h_tile((t + 1) % tiles)
                prv = h_tile((t - 1) % tiles)
                east = jnp.where(lane < LANES - 1, pltpu.roll(h, LANES - 1, 1), pltpu.roll(nxt, LANES - 1, 1))
                west = jnp.where(lane > 0, pltpu.roll(h, 1, 1), pltpu.roll(prv, 1, 1))
                h_dx = (pltpu.roll(h, height - 1, 0) - pltpu.roll(h, 1, 0)) * 0.5
                h_dy = (east - west) * 0.5
                u = ext[m, 1, :, cols_of(t)]
                v = ext[m, 2, :, cols_of(t)]
                u1 = u + DT * (CORIOLIS * v - h_dx)
                v1 = v + DT * (-CORIOLIS * u - h_dy)
                ext[m, 1, :, cols_of(t)] = u1
                ext[m, 2, :, cols_of(t)] = v1
                gbuf[:, cols_of(t)] = dep[:, cols_of(t)] * v1
            for t in range(tiles):
                g = g_tile(t)
                nxt = g_tile((t + 1) % tiles)
                prv = g_tile((t - 1) % tiles)
                east = jnp.where(lane < LANES - 1, pltpu.roll(g, LANES - 1, 1), pltpu.roll(nxt, LANES - 1, 1))
                west = jnp.where(lane > 0, pltpu.roll(g, 1, 1), pltpu.roll(prv, 1, 1))
                f = dep[:, cols_of(t)] * ext[m, 1, :, cols_of(t)]
                f_dx = (pltpu.roll(f, height - 1, 0) - pltpu.roll(f, 1, 0)) * 0.5
                g_dy = (east - west) * 0.5
                ext[m, 0, :, cols_of(t)] = h_tile(t) - DT * (f_dx + g_dy)
            return carry

        lax.fori_loop(0, STEPS, step_body, 0)
        for f in range(fields):
            for t in range(tiles):
                out_ref[t, m, f] = ext[m, f, pl.ds(HALO, rows), cols_of(t)]
        block = 256
        turned = jnp.concatenate(
            [jnp.transpose(jnp.concatenate([ext[m, 0, pl.ds(HALO, rows), cols_of(t)] for t in range(4 * g, 4 * g + 4)], 0))
             for g in range(tiles // 4)], 1)
        hi = turned.astype(BF16)
        rest = turned - hi.astype(F32)
        mid = rest.astype(BF16)
        low = (rest - mid.astype(F32)).astype(BF16)
        parts = jnp.concatenate([hi, mid, low], 0)
        for q in range(nobs // block):
            span = slice(q * block, (q + 1) * block)
            hot = jnp.where(iota((tiles * rows, block), 0) == combo[:, span], 1.0, 0.0).astype(BF16)
            picked = nn(parts, hot)
            picked = picked[0:LANES] + picked[LANES:2 * LANES] + picked[2 * LANES:]
            got = jnp.sum(jnp.where(iota((LANES, block), 0) == lane_of[:, span], picked, 0.0), 0, keepdims=True)
            for s in range(block // LANES):
                mine[pl.ds(m * 8 + q * (block // LANES) + s, 1), :] = got[:, s * LANES:(s + 1) * LANES]
        return 0

    lax.fori_loop(0, members, member_body, 0)

    part[sub] = mine[...]
    first = []
    for k in range(1, n_sub):
        cp = pltpu.make_async_remote_copy(
            mine, part.at[sub], s1_sem.at[k], r1_sem.at[k],
            device_id=(me, lax.rem(sub + k, n_sub)), device_id_type=MESH)
        cp.start()
        first.append(cp)
    for cp in first:
        cp.wait()
    total = part[0]
    for k in range(1, n_sub):
        total = total + part[k]
    slots[...] = total
    prior_ref[me] = total
    second = []
    for k in range(1, n_mem):
        cp = pltpu.make_async_remote_copy(
            slots, prior_ref.at[me], s2_sem.at[k], r2_sem.at[k],
            device_id=(lax.rem(me + k, n_mem), sub), device_id_type=MESH)
        cp.start()
        second.append(cp)
    for cp in second:
        cp.wait()


def forecast(ensemble, sea_depth, cutoff, obs_xy):
    members, fields, rows, cols = ensemble.shape
    n_mem = lax.axis_size("mem")
    n_sub = lax.axis_size("sub")
    nobs = obs_xy.shape[1]
    tiles = cols // LANES
    width = members * 8 + nobs // LANES
    vmem = pl.BlockSpec(memory_space=pltpu.VMEM)
    hbm = pl.BlockSpec(memory_space=pl.ANY)
    dma = pltpu.SemaphoreType.DMA
    return pl.pallas_call(
        forecast_kernel,
        out_shape=(
            jax.ShapeDtypeStruct((tiles, members, fields, rows, LANES), F32),
            jax.ShapeDtypeStruct((n_mem, width, LANES), F32),
        ),
        in_specs=[hbm, hbm, vmem, vmem],
        out_specs=(vmem, vmem),
        scratch_shapes=[
            pltpu.VMEM((members, fields, rows + 2 * HALO, cols), F32),
            pltpu.VMEM((rows + 2 * HALO, cols), F32),
            pltpu.VMEM((rows + 2 * HALO, cols), F32),
            pltpu.VMEM((n_sub, width, LANES), F32),
            pltpu.VMEM((width, LANES), F32),
            pltpu.VMEM((width, LANES), F32),
            dma((members + 1,)), dma((2, members)), dma((2, members)), dma((2,)), dma((2,)),
            dma((n_sub,)), dma((n_sub,)), dma((n_mem,)), dma((n_mem,)),
        ],
        compiler_params=pltpu.CompilerParams(
            collective_id=0, has_side_effects=True, vmem_limit_bytes=56 << 20),
        name="forecast",
    )(ensemble, sea_depth, cutoff, obs_xy)


def weights_kernel(prior_ref, obs_ref, val_ref, var_ref, at_ref, wt_ref, flat, heights, cuts, *, size_x, size_y):
    n_mem, width, _ = prior_ref.shape
    batches, members, nobs = at_ref.shape
    per = members // n_mem
    groups = batches * nobs // LANES
    flat[...] = prior_ref[:, 0:per * 8, :].reshape(members * 8, LANES)
    cut = jnp.sum(prior_ref[:, per * 8:per * 8 + groups, :], 0)
    for q in range(groups):
        b, s = q * LANES // nobs, q * LANES % nobs
        heights[b, :, s:s + LANES] = flat[pl.ds(q, members, stride=8), :]
        cuts[b, :, s:s + LANES] = cut[q:q + 1, :]
    scale = 1.0 / (members - 1)

    def batch_body(b, _):
        h = heights[b]
        mean = jnp.mean(h, 0, keepdims=True)
        at = h - mean
        inv_var = 1.0 / var_ref[b]
        scaled = at * inv_var
        gram = nt(scaled, at, HIGHEST) * scale
        eye = jnp.where(iota((members, members), 0) == iota((members, members), 1), 1.0, 0.0)
        aug = jnp.concatenate([gram + eye, eye], 1)

        def eliminate(g, x):
            for j in range(8):
                col = jnp.broadcast_to(x[:, j:j + 1], x.shape)
                row = x[j:j + 1, :] / col[j:j + 1, :]
                fixed = x - col * row
                x = jnp.where(iota(x.shape, 0) == j, row, fixed)
            x = jnp.concatenate([x[8:], x[:8]], 0)
            return pltpu.roll(x, x.shape[1] - 8, 1)

        aug = lax.fori_loop(0, members // 8, eliminate, aug)
        inverse = aug[:, 0:members]
        big = nn(inverse, scaled, HIGHEST)
        gap = (val_ref[b] - mean) * inv_var
        lean = jnp.sum(at * gap, 1, keepdims=True)
        small = gap - scale * jnp.sum(big * lean, 0, keepdims=True)
        wt = small - 0.5 * big
        at_ref[b] = at * scale
        wt_ref[b] = wt

        xy = jnp.transpose(jnp.broadcast_to(obs_ref[b, 0:1, :].astype(F32), (8, nobs)))
        yy = jnp.transpose(jnp.broadcast_to(obs_ref[b, 1:2, :].astype(F32), (8, nobs)))
        from_x = xy[:, 0:1]
        from_y = yy[:, 0:1]
        anom = jnp.transpose(at * scale)

        def carry_body(c, _):
            hc = heights[c]
            dev = hc - jnp.mean(hc, 0, keepdims=True)
            cross = nn(anom, dev, HIGHEST)
            gx = jnp.abs(obs_ref[c, 0:1, :].astype(F32) - from_x)
            gx = jnp.minimum(gx, size_x - gx)
            gy = jnp.abs(obs_ref[c, 1:2, :].astype(F32) - from_y)
            gy = jnp.minimum(gy, size_y - gy)
            radius = cuts[c]
            near = jnp.maximum(1.0 - (gx * gx + gy * gy) / (radius * radius), 0.0)
            heights[c] = hc + nn(wt, cross * (near * near), HIGHEST)
            return 0

        lax.fori_loop(b + 1, batches, carry_body, 0)
        return 0

    lax.fori_loop(0, batches, batch_body, 0)


def weights(prior, obs, values, variance, members, size_x, size_y):
    batches, _, nobs = obs.shape
    vmem = pl.BlockSpec(memory_space=pltpu.VMEM)
    return pl.pallas_call(
        functools.partial(weights_kernel, size_x=float(size_x), size_y=float(size_y)),
        out_shape=(jax.ShapeDtypeStruct((batches, members, nobs), F32),) * 2,
        in_specs=[vmem] * 4,
        out_specs=(vmem, vmem),
        scratch_shapes=[
            pltpu.VMEM((members * 8, LANES), F32),
            pltpu.VMEM((batches, members, nobs), F32),
            pltpu.VMEM((batches, 1, nobs), F32),
        ],
        compiler_params=pltpu.CompilerParams(vmem_limit_bytes=16 << 20),
        cost_estimate=pl.CostEstimate(flops=200_000_000, bytes_accessed=2_000_000, transcendentals=0),
        name="weights",
    )(prior, obs, values, variance)


def update_kernel(state_ref, at_ref, wt_ref, obs_ref, cut_ref, out_ref,
                  lhs1, lhs2, far_x, sq_y, inv_r2, work, rhs1, rhs2, counts):
    members, fields, block, _ = state_ref.shape
    batches, _, nobs = at_ref.shape
    rows = cut_ref.shape[0]
    step = pl.program_id(0)
    size_x = rows * lax.axis_size("sub")
    size_y = LANES * lax.axis_size("mem")
    x0 = lax.axis_index("sub") * rows
    y0 = lax.axis_index("mem") * LANES

    @pl.when(step == 0)
    def _():
        cut = cut_ref[...].astype(F32)
        inv_r2[...] = 1.0 / (cut * cut)
        top = jnp.max(cut_ref[...])
        reach = top * top
        upper = jnp.where(iota((nobs, nobs), 0) < iota((nobs, nobs), 1), 1.0, 0.0).astype(BF16)

        def gap_to(pos, low, length, size):
            before = low - pos
            before = jnp.where(before < 0, before + size, before)
            after = pos - (low + length - 1)
            after = jnp.where(after < 0, after + size, after)
            inside = (pos >= low) & (pos < low + length)
            return jnp.where(inside, 0, jnp.minimum(before, after))

        def select(b, _):
            ox = obs_ref[b, 0:1, :]
            oy = obs_ref[b, 1:2, :]
            gx = gap_to(ox, x0, rows, size_x)
            gy = gap_to(oy, y0, LANES, size_y)
            keep = jnp.where(gx * gx + gy * gy < reach, 1.0, 0.0)
            rank = nn(jnp.broadcast_to(keep, (16, nobs)).astype(BF16), upper)[0:1]
            rank = jnp.where(keep > 0.5, rank, -1.0)
            total = jnp.sum(keep).astype(jnp.int32)
            chunks = (total + CHUNK - 1) // CHUNK
            counts[b] = chunks
            a_hi, a_lo = split2(at_ref[b])
            w_hi, w_lo = split2(wt_ref[b])
            a3 = jnp.concatenate([a_hi, a_hi, a_lo], 0)
            w2 = jnp.concatenate([w_hi, w_lo], 1)

            def pack(c, _):
                want = (iota((CHUNK, nobs), 0) + c * CHUNK).astype(F32)
                hot = jnp.where(rank == want, 1.0, 0.0)
                hot16 = hot.astype(BF16)
                lhs1[b, c] = nt(hot16, a3).astype(BF16)
                zero = jnp.zeros_like(hot16)
                turn = jnp.concatenate(
                    [jnp.concatenate([hot16, hot16, zero], 0), jnp.concatenate([zero, zero, hot16], 0)], 1)
                lhs2[b, c] = nt(w2, turn).astype(BF16)
                px = jnp.sum(hot * ox.astype(F32), 1, keepdims=True)
                py = jnp.sum(hot * oy.astype(F32), 1, keepdims=True)
                far_x[b, c] = jnp.broadcast_to(px, (CHUNK, LANES))
                gy = jnp.abs((iota((CHUNK, LANES), 1) + y0).astype(F32) - py)
                gy = jnp.minimum(gy, size_y - gy)
                sq_y[b, c] = gy * gy
                return 0

            lax.fori_loop(0, chunks, pack, 0)
            return 0

        lax.fori_loop(0, batches, select, 0)

    slabs = fields * block
    source = state_ref.reshape(members * slabs, LANES)
    target = out_ref.reshape(members * slabs, LANES)
    for s in range(slabs):
        work[:, s * LANES:(s + 1) * LANES] = source[pl.ds(s, members, stride=slabs), :]

    def batch_body(b, _):
        for s in range(slabs):
            span = slice(s * LANES, (s + 1) * LANES)
            x = work[:, span]
            hi, lo = split2(x - jnp.mean(x, 0, keepdims=True))
            rhs1[0:members, span] = hi
            rhs1[members:2 * members, span] = lo
            rhs1[2 * members:, span] = hi

        def chunk_body(c, _):
            left = lhs1[b, c]
            right = lhs2[b, c]
            px = far_x[b, c]
            dy = sq_y[b, c]
            for r in range(0, block, 2):
                near = []
                for k in (r, r + 1):
                    row = step * block + k
                    gx = jnp.abs(px - (x0 + row).astype(F32))
                    gx = jnp.minimum(gx, size_x - gx)
                    ratio = (gx * gx + dy) * inv_r2[pl.ds(row, 1), :]
                    part = jnp.maximum(1.0 - ratio, 0.0)
                    near.append(part * part)
                near = jnp.concatenate(near, 1)
                for f in range(fields):
                    s = f * block + r
                    span = slice(s * LANES, (s + 2) * LANES)
                    hi, lo = split2(nn(left, rhs1[:, span]) * near)
                    work[:, span] += nn(right, jnp.concatenate([hi, lo, hi], 0))
            return 0

        lax.fori_loop(0, counts[b], chunk_body, 0)
        return 0

    lax.fori_loop(0, batches, batch_body, 0)
    for s in range(slabs):
        target[pl.ds(s, members, stride=slabs), :] = work[:, s * LANES:(s + 1) * LANES]


def update(state, at, wt, obs, cutoff):
    members, fields, rows, _ = state.shape
    batches, _, nobs = at.shape
    block = 8
    chunks = nobs // CHUNK
    whole = pl.BlockSpec((members, fields, block, LANES), lambda i: (0, 0, i, 0))
    vmem = pl.BlockSpec(memory_space=pltpu.VMEM)
    width = fields * block * LANES
    return pl.pallas_call(
        update_kernel,
        out_shape=jax.ShapeDtypeStruct(state.shape, F32),
        grid=(rows // block,),
        in_specs=[whole, vmem, vmem, vmem, vmem],
        out_specs=whole,
        scratch_shapes=[
            pltpu.VMEM((batches, chunks, CHUNK, 3 * members), BF16),
            pltpu.VMEM((batches, chunks, members, 3 * CHUNK), BF16),
            pltpu.VMEM((batches, chunks, CHUNK, LANES), F32),
            pltpu.VMEM((batches, chunks, CHUNK, LANES), F32),
            pltpu.VMEM((rows, LANES), F32),
            pltpu.VMEM((members, width), F32),
            pltpu.VMEM((3 * members, width), BF16),
            pltpu.VMEM((3 * CHUNK, width), BF16),
            pltpu.SMEM((batches,), jnp.int32),
        ],
        compiler_params=pltpu.CompilerParams(vmem_limit_bytes=40 << 20),
        name="update",
    )(state, at, wt, obs, cutoff)


def local(ensemble, sea_depth, cutoff, obs_index, obs_value, obs_var):
    per, fields, rows, cols = ensemble.shape
    members = per * lax.axis_size("mem")
    size_x = rows * lax.axis_size("sub")
    obs_x = obs_index // cols
    obs_y = obs_index % cols
    obs = jnp.stack([obs_x, obs_y], 1)
    flat = jnp.stack([obs_x.reshape(-1), obs_y.reshape(-1)], 0)
    blocks, prior = forecast(ensemble, sea_depth, cutoff, flat)
    state = lax.all_to_all(
        blocks.reshape(cols // LANES, per * fields * rows, LANES), "mem", split_axis=0, concat_axis=0, tiled=True)
    at, wt = weights(prior, obs, obs_value[:, None, :], obs_var[:, None, :], members, size_x, cols)
    return update(state.reshape(members, fields, rows, LANES), at, wt, obs, cutoff)


def solution(mesh):
    return jax.shard_map(
        local,
        mesh=mesh,
        in_specs=(P("mem", None, "sub", None), P("sub", None), P("sub", "mem"), P(), P(), P()),
        out_specs=P(None, None, "sub", "mem"),
        check_vma=False,
    )
```

time: 1240 us -> 148 us (0.12)
  waiting for transfers between devices: 559 us -> 14.3 us
  other arithmetic: 300 us -> 1.32 us
  local copies, waits for them, and re-layouts: 185 us -> 2.66 us
  matrix products: 132 us -> 0 us
  Pallas kernels: 0 us -> 122 us
  starting transfers between devices: 33.5 us -> 5.21 us
  between operations: 19.3 us -> 0.14 us
    psum x4 -> x0, waiting for transfers between devices: 549 us -> none  [local(): prior_obs = lax.psum(local_part, ('mem', 'sub'))]
    another operation x38 -> x2, other arithmetic: 239 us -> 0.62 us  [the longest x1 0.61 us: local(): flat = jnp.stack([obs_x.reshape(-1), obs_y.reshape(-1)], 0)]
    pallas_call x0 -> x3, Pallas kernels: none -> 122 us  [the longest x1 50.5 us: forecast(): pl.pallas_call(forecast_kernel, out_shape=(jax.ShapeDtypeStruct((tiles, m...]
    dot_general x16 -> x0, matrix products: 102 us -> none  [the longest x4 54.3 us: update_state(): jnp.dot(obs_anom, state_anom, precision=highest) / (member_count - 1)]
    mul x8 -> x0, local copies, waits for them, and re-layouts: 79.6 us -> none  [update_state(): cross_cov.reshape(obs_count, 3, cell_count) * loc_weight[:, None, :]]
    unnamed x76 -> x14, local copies, waits for them, and re-layouts: 41 us -> 2.64 us
    another operation x38 -> x2, local copies, waits for them, and re-layouts: 36.8 us -> 0.01 us  [local(): obs = jnp.stack([obs_x, obs_y], 1)]
    another operation x32 -> x0, matrix products: 30.3 us -> none  [the longest x24 19.2 us: analysis_weights(): solved = jax.scipy.linalg.cho_solve((factor, True), right_side)]
  transfers between devices with their start and end apart: 21 -> 1, of which waited for: 18 -> 1; matrix products, arithmetic and copies ran while one was open for 8% -> 0% of each run, Pallas kernels for 0% -> 20%
where the time goes in v1:
time: 148 us; the launch traced here: 146 us
  Pallas kernels  122 us (82%)
  waiting for transfers between devices  14.3 us (10%)
  starting transfers between devices  5.21 us (4%)
  local copies, waits for them, and re-layouts  2.66 us (2%)
    pallas_call x1, Pallas kernels, forecast(): pl.pallas_call(forecast_kernel, out_shape=(jax.ShapeDtypeStruct((tiles, m...  50.5 us
    pallas_call x1, Pallas kernels, update(): pl.pallas_call(update_kernel, out_shape=jax.ShapeDtypeStruct(state.shape,...  42 us
    pallas_call x1, Pallas kernels, weights(): pl.pallas_call(functools.partial(weights_kernel, size_x=float(size_x), si...  29.9 us
    all_to_all x1, waiting for transfers between devices, local(): lax.all_to_all(blocks.reshape(cols // LANES, per * fields * rows, LANES),...  14.3 us
    all_to_all x1, starting transfers between devices, local(): lax.all_to_all(blocks.reshape(cols // LANES, per * fields * rows, LANES),...  5.21 us
  transfers between devices with their start and end apart: 1, of which 1 were waited for; matrix products, arithmetic and copies ran while one was open for 0% of the time, Pallas kernels for 20%

profile of v1, /device:TPU:1, one launch (start us, length us, event | category | flops | bytes accessed | tf_op | source)
XLA Modules:
  0.0 146.0 jit_solution(11549592583283042377)
XLA Ops:
  0.0 0.7 add_select_fusion.1
  0.7 0.6 pad_add_fusion.obs_ref
  1.3 50.5 %forecast.1 = (f32[16,4,3,32,128]{4,3,2,1,0:T(8,128)}, f32[16,40,128]{2,1,0:T(8,128)}) custom-call(f32[4,3,32,2048]{3,2,1,0:T(8,128)} %ens_ref.1, f32[32,2048]{1,0:T(8,128)} %depth_ref.1, s32[32,128]{1,0:T(8,128)} %cut_ref.3, s32[2,1024]{1,0:T(2,128)} %pad_add_fusion.obs_ref), custom_call_target="tpu_custom_call" | custom-call | tf_op jit(solution)/shard_map/forecast/pallas_call | solution.py:216
  51.9 0.0 copy-start.4
  51.9 0.0 copy-start.5
  51.9 0.0 copy-start.2
  51.9 5.2 %all-to-all-start = ((f32[16,384,128]{2,1,0:T(8,128)}), f32[16,384,128]{2,1,0:T(8,128)S(1)}, u32[]{:S(2)}, u32[]{:S(2)}) async-start(f32[16,384,128]{2,1,0:T(8,128)} %bitcast.10), calls=%async_computation | async-start | bytes 6291456 | tf_op jit(solution)/shard_map/all_to_all | solution.py:475
  57.2 0.0 copy-done.4
  57.2 0.0 copy-done.5
  57.2 0.0 copy-start.3
  57.2 1.0 copy-done.3
  58.2 29.9 %weights.1 = (f32[4,64,256]{2,1,0:T(8,128)S(1)}, f32[4,64,256]{2,1,0:T(8,128)S(1)}) custom-call(f32[16,40,128]{2,1,0:T(8,128)S(1)} %copy-done.3, s32[4,2,256]{2,1,0:T(2,128)S(1)} %pad_add_fusion.1.obs_ref, f32[4,1,256]{2,1,0:T(1,128)S(1)} %broadcast_in_dim.6.val_ref, f32[4,1,256]{2,1,0:T(1,128)S(1)} %broadcast_in_dim.7.var_ref), custom_call_target="tpu_custom_call" | custom-call | flops 200000000 | bytes 2000000 | tf_op jit(solution)/shard_map/weights/pallas_call | solution.py:310
  88.1 0.0 copy-start
  88.1 0.7 copy-done
  88.8 14.3 %all-to-all-done = f32[16,384,128]{2,1,0:T(8,128)S(1)} async-done(((f32[16,384,128]{2,1,0:T(8,128)}), f32[16,384,128]{2,1,0:T(8,128)S(1)}, u32[]{:S(2)}, u32[]{:S(2)}) %all-to-all-start) | async-done | bytes 3145760 | tf_op jit(solution)/shard_map/all_to_all | solution.py:475
  103.0 0.0 copy-done.2
  103.0 0.0 copy-start.1
  103.0 0.9 copy-done.1
  104.0 42.0 %update.1 = f32[64,3,32,128]{3,2,1,0:T(8,128)} custom-call(f32[64,3,32,128]{3,2,1,0:T(8,128)S(1)} %bitcast.9, f32[4,64,256]{2,1,0:T(8,128)S(1)} %get-tuple-element.11.at_ref, f32[4,64,256]{2,1,0:T(8,128)S(1)} %copy-done.1, s32[4,2,256]{2,1,0:T(2,128)S(1)} %pad_add_fusion.1.obs_ref, s32[32,128]{1,0:T(8,128)S(1)} %copy-done.2), custom_call_target="tpu_custom_call" | custom-call | tf_op jit(solution)/shard_map/update/pallas_call | solution.py:444
  (7 shorter events, 0.0 us)
Async XLA Ops:
  51.9 5.3 %copy-start.4 = (f32[4,256]{1,0:T(4,128)S(1)}, f32[4,256]{1,0:T(4,128)}, u32[]{:S(2)}) copy-start(f32[4,256]{1,0:T(4,128)} %param.10) | copy-start | bytes 12292
  51.9 5.3 %copy-start.5 = (f32[4,256]{1,0:T(4,128)S(1)}, f32[4,256]{1,0:T(4,128)}, u32[]{:S(2)}) copy-start(f32[4,256]{1,0:T(4,128)} %param.11) | copy-start | bytes 12292
  51.9 51.1 %copy-start.2 = (s32[32,128]{1,0:T(8,128)S(1)}, s32[32,128]{1,0:T(8,128)}, u32[]{:S(2)}) copy-start(s32[32,128]{1,0:T(8,128)} %cut_ref.3) | copy-start | bytes 49156
  51.9 51.1 %all-to-all-start = ((f32[16,384,128]{2,1,0:T(8,128)}), f32[16,384,128]{2,1,0:T(8,128)S(1)}, u32[]{:S(2)}, u32[]{:S(2)}) async-start(f32[16,384,128]{2,1,0:T(8,128)} %bitcast.10), calls=%async_computation | async-start | bytes 6291456 | tf_op jit(solution)/shard_map/all_to_all | solution.py:475
  57.2 1.0 copy-start.3
  88.1 0.7 copy-start
  103.0 1.0 copy-start.1

commit v2 on v1

v2 whole, which is shorter than its diff:
```python
import functools

import jax
import jax.numpy as jnp
from jax import lax
from jax.experimental import pallas as pl
from jax.experimental.pallas import tpu as pltpu
from jax.sharding import PartitionSpec as P

STEPS = 4
BATCHES = 4
DT = 0.3
CORIOLIS = 0.2
MESH = pl.DeviceIdType.MESH
HIGHEST = lax.Precision.HIGHEST
F32 = jnp.float32
BF16 = jnp.bfloat16
HALO = 8
CHUNK = 32
LANES = 128


def nt(a, b, precision=None):
    return lax.dot_general(
        a, b, (((1,), (1,)), ((), ())), precision=precision, preferred_element_type=F32
    )


def nn(a, b, precision=None):
    return lax.dot_general(
        a, b, (((1,), (0,)), ((), ())), precision=precision, preferred_element_type=F32
    )


def split2(x):
    hi = x.astype(BF16)
    return hi, (x - hi.astype(F32)).astype(BF16)


def iota(shape, dim):
    return lax.broadcasted_iota(jnp.int32, shape, dim)


SIDE = 4
ORDER = (
    (0, 1), (0, 3), (1, 0), (3, 0), (1, 1), (3, 3), (1, 3), (3, 1),
    (0, 2), (2, 0), (2, 1), (2, 3), (1, 2), (3, 2), (2, 2),
)
EARLY = 15


def forecast_kernel(
    ens_ref, depth_ref, cut_ref, obs_ref, batch_ref, val_ref, var_ref,
    out_ref, at_ref, wt_ref,
    ext, dep, hbuf, fbuf, gbuf, part, slots, mine, prior_ref, staged, flat, heights, cuts,
    lsem, hs_sem, hr_sem, ds_sem, dr_sem, s1_sem, r1_sem, s2_sem, r2_sem, bs_sem, br_sem, own_sem,
):
    members, fields, rows, cols = ens_ref.shape
    tiles = cols // LANES
    me = lax.axis_index("mem")
    sub = lax.axis_index("sub")
    n_mem = lax.axis_size("mem")
    n_sub = lax.axis_size("sub")
    nobs = obs_ref.shape[1]

    barrier = pltpu.get_barrier_semaphore()
    for k in range(1, n_sub):
        pl.semaphore_signal(barrier, inc=1, device_id=(me, lax.rem(sub + k, n_sub)), device_id_type=MESH)
    for k in range(1, n_mem):
        pl.semaphore_signal(barrier, inc=1, device_id=(lax.rem(me + k, n_mem), sub), device_id_type=MESH)

    local = []
    cp = pltpu.make_async_copy(depth_ref, dep.at[pl.ds(HALO, rows)], lsem.at[members])
    cp.start()
    local.append(cp)
    for m in range(members):
        cp = pltpu.make_async_copy(ens_ref.at[m], ext.at[m, :, pl.ds(HALO, rows)], lsem.at[m])
        cp.start()
        local.append(cp)
    pl.semaphore_wait(barrier, n_sub - 1 + n_mem - 1)

    up = lax.rem(sub + n_sub - 1, n_sub)
    down = lax.rem(sub + 1, n_sub)
    halo = []
    for d, (peer, src, dst) in enumerate(((up, 0, HALO + rows), (down, rows - HALO, 0))):
        cp = pltpu.make_async_remote_copy(
            depth_ref.at[pl.ds(src, HALO)], dep.at[pl.ds(dst, HALO)],
            ds_sem.at[d], dr_sem.at[d], device_id=(me, peer), device_id_type=MESH)
        cp.start()
        halo.append(cp)

    def halo_copies(m):
        return [
            pltpu.make_async_remote_copy(
                ens_ref.at[m, :, pl.ds(src, HALO)], ext.at[m, :, pl.ds(dst, HALO)],
                hs_sem.at[d, m], hr_sem.at[d, m], device_id=(me, peer), device_id_type=MESH)
            for d, (peer, src, dst) in enumerate(((up, 0, HALO + rows), (down, rows - HALO, 0)))
        ]

    for m in range(members):
        for cp in halo_copies(m):
            cp.start()

    obs_x = obs_ref[0:1, :]
    obs_y = obs_ref[1:2, :]
    local_x = obs_x - sub * rows
    in_rows = (local_x >= 0) & (local_x < rows)
    combo = jnp.where(in_rows, (obs_y // LANES) * rows + local_x, -1)
    lane_of = obs_y % LANES

    in_block = in_rows & (obs_y // LANES == me)
    pick_row = jnp.where(in_block, local_x, -1)
    cut_t = jnp.transpose(cut_ref[...].astype(F32))
    row_hot = jnp.where(iota((rows, nobs), 0) == pick_row, 1.0, 0.0)
    cut_cols = nn(cut_t.astype(BF16), row_hot.astype(BF16))
    cut_obs = jnp.sum(jnp.where(iota((LANES, nobs), 0) == lane_of, cut_cols, 0.0), 0, keepdims=True)
    for q in range(nobs // LANES):
        mine[pl.ds(members * 8 + q, 1), :] = cut_obs[:, q * LANES:(q + 1) * LANES]

    halo[0].wait()
    halo[1].wait()
    local[0].wait()

    height = rows + 2 * HALO
    lane = iota((height, LANES), 1)
    here, above, below = (pl.ds(HALO + k, height) for k in (0, 1, -1))
    pad = jnp.zeros((HALO, LANES), F32)
    for buf in (hbuf, fbuf):
        for t in range(tiles):
            buf[t, 0:HALO] = pad
            buf[t, HALO + height:] = pad

    def cols_of(t):
        return pl.ds(t * LANES, LANES)

    def spread(load):
        first_east = pltpu.roll(load(0), LANES - 1, 1)
        east = first_east
        west_before = pltpu.roll(load(tiles - 1), 1, 1)
        for t in range(tiles):
            east_next = first_east if t == tiles - 1 else pltpu.roll(load(t + 1), LANES - 1, 1)
            west = pltpu.roll(load(t), 1, 1)
            yield t, jnp.where(lane < LANES - 1, east, east_next) - jnp.where(lane > 0, west, west_before)
            east, west_before = east_next, west

    half = 0.5 * DT

    def block_copies(m, first, last):
        found = []
        for n, (dz, dx) in list(enumerate(ORDER))[first:last]:
            peer = lax.rem(me // SIDE + dz, SIDE) * SIDE + lax.rem(lax.rem(me, SIDE) + dx, SIDE)
            found.append(pltpu.make_async_remote_copy(
                staged.at[peer, m], out_ref.at[me, m], bs_sem.at[n, m], br_sem.at[n, m],
                device_id=(peer, sub), device_id_type=MESH))
        return found

    def own_copy(m):
        return pltpu.make_async_copy(staged.at[me, m], out_ref.at[me, m], own_sem.at[m])

    def member_body(m, _):
        pltpu.make_async_copy(ens_ref.at[m], ext.at[m, :, pl.ds(HALO, rows)], lsem.at[m]).wait()
        for cp in halo_copies(m):
            cp.wait()
        for t in range(tiles):
            hbuf[t, here] = ext[m, 0, :, cols_of(t)]

        def step_body(s, carry):
            for t, h_dy in spread(lambda t: hbuf[t, here]):
                u = ext[m, 1, :, cols_of(t)]
                v = ext[m, 2, :, cols_of(t)]
                u1 = u + ((DT * CORIOLIS) * v - half * (hbuf[t, above] - hbuf[t, below]))
                v1 = v - ((DT * CORIOLIS) * u + half * h_dy)
                d = dep[:, cols_of(t)]
                ext[m, 1, :, cols_of(t)] = u1
                ext[m, 2, :, cols_of(t)] = v1
                fbuf[t, here] = d * u1
                gbuf[t] = d * v1
            for t, g_dy in spread(lambda t: gbuf[t]):
                hbuf[t, here] = hbuf[t, here] - half * (fbuf[t, above] - fbuf[t, below] + g_dy)
            return carry

        lax.fori_loop(0, STEPS, step_body, 0)
        inner = pl.ds(2 * HALO, rows)
        for t in range(tiles):
            staged[t, m, 0] = hbuf[t, inner]
            for f in range(1, fields):
                staged[t, m, f] = ext[m, f, pl.ds(HALO, rows), cols_of(t)]
        own_copy(m).start()

        @pl.when(m == 0)
        def _():
            for cp in block_copies(m, 0, EARLY):
                cp.start()

        block = 256
        turned = jnp.concatenate(
            [jnp.transpose(jnp.concatenate([hbuf[t, inner] for t in range(4 * g, 4 * g + 4)], 0))
             for g in range(tiles // 4)], 1)
        hi = turned.astype(BF16)
        rest = turned - hi.astype(F32)
        mid = rest.astype(BF16)
        low = (rest - mid.astype(F32)).astype(BF16)
        parts = jnp.concatenate([hi, mid, low], 0)
        for q in range(nobs // block):
            span = slice(q * block, (q + 1) * block)
            hot = jnp.where(iota((tiles * rows, block), 0) == combo[:, span], 1.0, 0.0).astype(BF16)
            picked = nn(parts, hot)
            picked = picked[0:LANES] + picked[LANES:2 * LANES] + picked[2 * LANES:]
            got = jnp.sum(jnp.where(iota((LANES, block), 0) == lane_of[:, span], picked, 0.0), 0, keepdims=True)
            for s in range(block // LANES):
                mine[pl.ds(m * 8 + q * (block // LANES) + s, 1), :] = got[:, s * LANES:(s + 1) * LANES]
        return 0

    lax.fori_loop(0, members, member_body, 0)

    part[sub] = mine[...]
    first = []
    for k in range(1, n_sub):
        cp = pltpu.make_async_remote_copy(
            mine, part.at[sub], s1_sem.at[k], r1_sem.at[k],
            device_id=(me, lax.rem(sub + k, n_sub)), device_id_type=MESH)
        cp.start()
        first.append(cp)
    for cp in first:
        cp.wait()
    total = part[0]
    for k in range(1, n_sub):
        total = total + part[k]
    slots[...] = total
    prior_ref[me] = total
    second = []
    for k in range(1, n_mem):
        cp = pltpu.make_async_remote_copy(
            slots, prior_ref.at[me], s2_sem.at[k], r2_sem.at[k],
            device_id=(lax.rem(me + k, n_mem), sub), device_id_type=MESH)
        cp.start()
        second.append(cp)
    for cp in block_copies(0, EARLY, len(ORDER)):
        cp.start()

    def rest_body(m, _):
        for cp in block_copies(m, 0, len(ORDER)):
            cp.start()
        return 0

    lax.fori_loop(1, members, rest_body, 0)
    for cp in second:
        cp.wait()
    weights(prior_ref, batch_ref, val_ref, var_ref, at_ref, wt_ref, flat, heights, cuts,
            float(rows * n_sub), float(cols))

    def finish_body(m, _):
        for cp in block_copies(m, 0, len(ORDER)):
            cp.wait()
        own_copy(m).wait()
        return 0

    lax.fori_loop(0, members, finish_body, 0)


def nn3(a, b):
    a_hi, a_lo = split2(a)
    b_hi, b_lo = split2(b)
    return nn(a_hi, b_hi) + (nn(a_hi, b_lo) + nn(a_lo, b_hi))


def weights(prior_ref, obs_ref, val_ref, var_ref, at_ref, wt_ref, flat, heights, cuts, size_x, size_y):
    n_mem, width, _ = prior_ref.shape
    batches, members, nobs = at_ref.shape
    per = members // n_mem
    groups = batches * nobs // LANES
    flat[...] = prior_ref[:, 0:per * 8, :].reshape(members * 8, LANES)
    cut = jnp.sum(prior_ref[:, per * 8:per * 8 + groups, :], 0)
    cut = 1.0 / (cut * cut)
    for q in range(groups):
        b, s = q * LANES // nobs, q * LANES % nobs
        heights[b, :, s:s + LANES] = flat[pl.ds(q, members, stride=8), :]
        cuts[b, :, s:s + LANES] = cut[q:q + 1, :]
    scale = 1.0 / (members - 1)

    def batch_body(b, _):
        h = heights[b]
        mean = jnp.mean(h, 0, keepdims=True)
        at = h - mean
        inv_var = 1.0 / var_ref[b]
        scaled = at * inv_var
        gram = nt(scaled, at, HIGHEST) * scale
        eye = jnp.where(iota((members, members), 0) == iota((members, members), 1), 1.0, 0.0)
        aug = jnp.concatenate([gram + eye, eye], 1)

        def eliminate(g, x):
            for j in range(0, 8, 2):
                col0 = jnp.broadcast_to(x[:, j:j + 1], x.shape)
                col1 = jnp.broadcast_to(x[:, j + 1:j + 2], x.shape)
                a, b01, c = col0[j:j + 1], col1[j:j + 1], col1[j + 1:j + 2]
                inv = 1.0 / (a * c - b01 * b01)
                row0 = (c * x[j:j + 1] - b01 * x[j + 1:j + 2]) * inv
                row1 = (a * x[j + 1:j + 2] - b01 * x[j:j + 1]) * inv
                fixed = x - col0 * row0 - col1 * row1
                x = jnp.where(iota(x.shape, 0) == j, row0, jnp.where(iota(x.shape, 0) == j + 1, row1, fixed))
            x = jnp.concatenate([x[8:], x[:8]], 0)
            return pltpu.roll(x, x.shape[1] - 8, 1)

        aug = lax.fori_loop(0, members // 8, eliminate, aug)
        inverse = aug[:, 0:members]
        big = nn(inverse, scaled, HIGHEST)
        gap = (val_ref[b] - mean) * inv_var
        lean = jnp.sum(at * gap, 1, keepdims=True)
        small = gap - scale * jnp.sum(big * lean, 0, keepdims=True)
        wt = small - 0.5 * big
        at_ref[b] = at * scale
        wt_ref[b] = wt

        xy = jnp.concatenate([jnp.broadcast_to(obs_ref[b, k:k + 1, :].astype(F32), (4, nobs)) for k in range(2)], 0)
        xy = jnp.transpose(xy)
        from_x = xy[:, 0:1]
        from_y = xy[:, 4:5]
        anom_hi, anom_lo = split2(jnp.transpose(at * scale))
        wt_hi, wt_lo = split2(wt)

        def carry_body(c, _):
            hc = heights[c]
            dev_hi, dev_lo = split2(hc - jnp.mean(hc, 0, keepdims=True))
            cross = nn(anom_hi, dev_hi) + (nn(anom_hi, dev_lo) + nn(anom_lo, dev_hi))
            gx = jnp.abs(obs_ref[c, 0:1, :].astype(F32) - from_x)
            gx = jnp.minimum(gx, size_x - gx)
            gy = jnp.abs(obs_ref[c, 1:2, :].astype(F32) - from_y)
            gy = jnp.minimum(gy, size_y - gy)
            near = jnp.maximum(1.0 - (gx * gx + gy * gy) * cuts[c], 0.0)
            gain_hi, gain_lo = split2(cross * (near * near))
            heights[c] = hc + (nn(wt_hi, gain_hi) + (nn(wt_hi, gain_lo) + nn(wt_lo, gain_hi)))
            return 0

        lax.fori_loop(b + 1, batches, carry_body, 0)
        return 0

    lax.fori_loop(0, batches, batch_body, 0)


def forecast(ensemble, sea_depth, cutoff, obs_xy, obs, values, variance):
    per, fields, rows, cols = ensemble.shape
    n_mem = lax.axis_size("mem")
    n_sub = lax.axis_size("sub")
    members = per * n_mem
    batches, _, nobs = obs.shape
    total = batches * nobs
    tiles = cols // LANES
    width = per * 8 + total // LANES
    vmem = pl.BlockSpec(memory_space=pltpu.VMEM)
    hbm = pl.BlockSpec(memory_space=pl.ANY)
    dma = pltpu.SemaphoreType.DMA
    vm = pltpu.VMEM
    return pl.pallas_call(
        forecast_kernel,
        out_shape=(
            jax.ShapeDtypeStruct((n_mem, per, fields, rows, LANES), F32),
            jax.ShapeDtypeStruct((batches, members, nobs), F32),
            jax.ShapeDtypeStruct((batches, members, nobs), F32),
        ),
        in_specs=[hbm, hbm] + [vmem] * 5,
        out_specs=(hbm, vmem, vmem),
        scratch_shapes=[
            vm((per, fields, rows + 2 * HALO, cols), F32),
            vm((rows + 2 * HALO, cols), F32),
            vm((tiles, rows + 4 * HALO, LANES), F32),
            vm((tiles, rows + 4 * HALO, LANES), F32),
            vm((tiles, rows + 2 * HALO, LANES), F32),
            vm((n_sub, width, LANES), F32),
            vm((width, LANES), F32),
            vm((width, LANES), F32),
            vm((n_mem, width, LANES), F32),
            vm((tiles, per, fields, rows, LANES), F32),
            vm((members * 8, LANES), F32),
            vm((batches, members, nobs), F32),
            vm((batches, 1, nobs), F32),
            dma((per + 1,)), dma((2, per)), dma((2, per)), dma((2,)), dma((2,)),
            dma((n_sub,)), dma((n_sub,)), dma((n_mem,)), dma((n_mem,)),
            dma((n_mem, per)), dma((n_mem, per)), dma((per,)),
        ],
        compiler_params=pltpu.CompilerParams(
            collective_id=0, has_side_effects=True, vmem_limit_bytes=56 << 20),
        name="forecast",
    )(ensemble, sea_depth, cutoff, obs_xy, obs, values, variance)


def update_kernel(state_ref, at_ref, wt_ref, obs_ref, cut_ref, out_ref,
                  lhs1, lhs2, far_x, sq_y, inv_r2, work, rhs1, begin, stage, counts, in_sems, sems):
    members, fields, rows, _ = state_ref.shape
    batches, _, nobs = at_ref.shape
    block = work.shape[1] // (fields * LANES)
    size_x = rows * lax.axis_size("sub")
    size_y = LANES * lax.axis_size("mem")
    x0 = lax.axis_index("sub") * rows
    y0 = lax.axis_index("mem") * LANES

    for step in range(rows // block):
        pltpu.make_async_copy(
            state_ref.at[:, :, pl.ds(step * block, block)], begin.at[step], in_sems.at[step]).start()
    cut = cut_ref[...].astype(F32)
    inv_r2[...] = 1.0 / (cut * cut)
    top = jnp.max(cut_ref[...])
    reach = top * top
    upper = jnp.where(iota((nobs, nobs), 0) < iota((nobs, nobs), 1), 1.0, 0.0).astype(BF16)

    def gap_to(pos, low, length, size):
        before = low - pos
        before = jnp.where(before < 0, before + size, before)
        after = pos - (low + length - 1)
        after = jnp.where(after < 0, after + size, after)
        inside = (pos >= low) & (pos < low + length)
        return jnp.where(inside, 0, jnp.minimum(before, after))

    def select(b, _):
        ox = obs_ref[b, 0:1, :]
        oy = obs_ref[b, 1:2, :]
        gx = gap_to(ox, x0, rows, size_x)
        gy = gap_to(oy, y0, LANES, size_y)
        keep = jnp.where(gx * gx + gy * gy < reach, 1.0, 0.0)
        rank = nn(jnp.broadcast_to(keep, (16, nobs)).astype(BF16), upper)[0:1]
        rank = jnp.where(keep > 0.5, rank, -1.0)
        total = jnp.sum(keep).astype(jnp.int32)
        chunks = (total + CHUNK - 1) // CHUNK
        counts[b] = chunks
        a = at_ref[b]
        a_hi, a_lo = split2(a - jnp.mean(a, 0, keepdims=True))
        w_hi, w_lo = split2(wt_ref[b])
        a3 = jnp.concatenate([a_hi, a_hi, a_lo], 0)
        w2 = jnp.concatenate([w_hi, w_lo], 1)

        def pack(c, _):
            want = (iota((CHUNK, nobs), 0) + c * CHUNK).astype(F32)
            hot = jnp.where(rank == want, 1.0, 0.0)
            hot16 = hot.astype(BF16)
            lhs1[b, c] = nt(hot16, a3).astype(BF16)
            zero = jnp.zeros_like(hot16)
            turn = jnp.concatenate(
                [jnp.concatenate([hot16, hot16, zero], 0), jnp.concatenate([zero, zero, hot16], 0)], 1)
            lhs2[b, c] = nt(w2, turn).astype(BF16)
            px = jnp.sum(hot * ox.astype(F32), 1, keepdims=True)
            py = jnp.sum(hot * oy.astype(F32), 1, keepdims=True)
            far_x[b, c] = jnp.broadcast_to(px, (CHUNK, LANES))
            gy = jnp.abs((iota((CHUNK, LANES), 1) + y0).astype(F32) - py)
            gy = jnp.minimum(gy, size_y - gy)
            sq_y[b, c] = gy * gy
            return 0

        lax.fori_loop(0, chunks, pack, 0)
        return 0

    lax.fori_loop(0, batches, select, 0)

    slabs = fields * block
    steps = rows // block

    def place(s):
        return pl.ds(s % fields * block + s // fields, members, stride=slabs)

    def part(step):
        return pl.ds(pl.multiple_of(step * block, block), block)

    def in_copy(step):
        return pltpu.make_async_copy(state_ref.at[:, :, part(step)], begin.at[step], in_sems.at[step])

    def out_copy(step):
        return pltpu.make_async_copy(stage.at[step], out_ref.at[:, :, part(step)], sems.at[step])

    def step_body(step, _):
        in_copy(step).wait()
        source = begin.at[step].reshape(members * slabs, LANES)
        target = stage.at[step].reshape(members * slabs, LANES)
        for s in range(slabs):
            work[:, s * LANES:(s + 1) * LANES] = source[place(s), :]

        def batch_body(b, _):
            for s in range(slabs):
                span = slice(s * LANES, (s + 1) * LANES)
                hi, lo = split2(work[:, span])
                rhs1[0:members, span] = hi
                rhs1[members:2 * members, span] = lo
                rhs1[2 * members:, span] = hi

            def chunk_body(c, _):
                left = lhs1[b, c]
                right = lhs2[b, c]
                px = far_x[b, c]
                dy = sq_y[b, c]
                for r in range(0, block, 2):
                    near = []
                    for k in (r, r + 1):
                        row = step * block + k
                        gx = jnp.abs(px - (x0 + row).astype(F32))
                        gx = jnp.minimum(gx, size_x - gx)
                        ratio = (gx * gx + dy) * inv_r2[pl.ds(row, 1), :]
                        part = jnp.maximum(1.0 - ratio, 0.0)
                        near += [part * part] * fields
                    near = jnp.concatenate(near, 1)
                    span = slice(r * fields * LANES, (r + 2) * fields * LANES)
                    hi, lo = split2(nn(left, rhs1[:, span]) * near)
                    work[:, span] += nn(right, jnp.concatenate([hi, lo, hi], 0))
                return 0

            lax.fori_loop(0, counts[b], chunk_body, 0)
            return 0

        lax.fori_loop(0, batches, batch_body, 0)
        for s in range(slabs):
            target[place(s), :] = work[:, s * LANES:(s + 1) * LANES]
        out_copy(step).start()
        return 0

    lax.fori_loop(0, steps, step_body, 0)
    for step in range(steps):
        out_copy(step).wait()


def update(state, at, wt, obs, cutoff):
    members, fields, rows, _ = state.shape
    batches, _, nobs = at.shape
    block = 8
    chunks = nobs // CHUNK
    vmem = pl.BlockSpec(memory_space=pltpu.VMEM)
    width = fields * block * LANES
    return pl.pallas_call(
        update_kernel,
        out_shape=jax.ShapeDtypeStruct(state.shape, F32),
        in_specs=[pl.BlockSpec(memory_space=pl.ANY)] + [vmem] * 4,
        out_specs=pl.BlockSpec(memory_space=pl.ANY),
        scratch_shapes=[
            pltpu.VMEM((batches, chunks, CHUNK, 3 * members), BF16),
            pltpu.VMEM((batches, chunks, members, 3 * CHUNK), BF16),
            pltpu.VMEM((batches, chunks, CHUNK, LANES), F32),
            pltpu.VMEM((batches, chunks, CHUNK, LANES), F32),
            pltpu.VMEM((rows, LANES), F32),
            pltpu.VMEM((members, width), F32),
            pltpu.VMEM((3 * members, width), BF16),
            pltpu.VMEM((rows // block, members, fields, block, LANES), F32),
            pltpu.VMEM((rows // block, members, fields, block, LANES), F32),
            pltpu.SMEM((batches,), jnp.int32),
            pltpu.SemaphoreType.DMA((rows // block,)),
            pltpu.SemaphoreType.DMA((rows // block,)),
        ],
        compiler_params=pltpu.CompilerParams(vmem_limit_bytes=40 << 20),
        name="update",
    )(state, at, wt, obs, cutoff)


def local(ensemble, sea_depth, cutoff, obs_index, obs_value, obs_var):
    per, fields, rows, cols = ensemble.shape
    members = per * lax.axis_size("mem")
    obs_x = obs_index // cols
    obs_y = obs_index % cols
    obs = jnp.stack([obs_x, obs_y], 1)
    flat = jnp.stack([obs_x.reshape(-1), obs_y.reshape(-1)], 0)
    state, at, wt = forecast(ensemble, sea_depth, cutoff, flat, obs, obs_value[:, None, :], obs_var[:, None, :])
    return update(state.reshape(members, fields, rows, LANES), at, wt, obs, cutoff)


def solution(mesh):
    return jax.shard_map(
        local,
        mesh=mesh,
        in_specs=(P("mem", None, "sub", None), P("sub", None), P("sub", "mem"), P(), P(), P()),
        out_specs=P(None, None, "sub", "mem"),
        check_vma=False,
    )
```

time: 148 us -> 95.2 us (0.64); the launches traced: 146 us -> 94.7 us
  Pallas kernels: 122 us -> 86.4 us
  waiting for transfers between devices: 14.3 us -> 0 us
  starting transfers between devices: 5.21 us -> 0 us
  local copies, waits for them, and re-layouts: 2.66 us -> 6.38 us
    pallas_call x1, Pallas kernels: 42 us -> 21.5 us  [update(): pl.pallas_call(update_kernel, out_shape=jax.ShapeDtypeStruct(state.shape,...]
    pallas_call x2 -> x1, Pallas kernels: 80.4 us -> 64.9 us  [forecast(): pl.pallas_call(forecast_kernel, out_shape=(jax.ShapeDtypeStruct((n_mem, p...]
    all_to_all x1 -> x0, waiting for transfers between devices: 14.3 us -> none  [local(): lax.all_to_all(blocks.reshape(cols // LANES, per * fields * rows, LANES),...]
    all_to_all x1 -> x0, starting transfers between devices: 5.21 us -> none  [local(): lax.all_to_all(blocks.reshape(cols // LANES, per * fields * rows, LANES),...]
    unnamed x14 -> x12, local copies, waits for them, and re-layouts: 2.64 us -> 3.8 us
  transfers between devices with their start and end apart: 1 -> 0, of which waited for: 1 -> 0; matrix products, arithmetic and copies ran while one was open for 0% -> 0% of each run, Pallas kernels for 20% -> 0%
where the time goes in v2:
time: 95.2 us; the launch traced here: 94.7 us
  Pallas kernels  86.4 us (91%)
  local copies, waits for them, and re-layouts  6.38 us (7%)
  other arithmetic  1.91 us (2%)
    pallas_call x1, Pallas kernels, forecast(): pl.pallas_call(forecast_kernel, out_shape=(jax.ShapeDtypeStruct((n_mem, p...  64.9 us
    pallas_call x1, Pallas kernels, update(): pl.pallas_call(update_kernel, out_shape=jax.ShapeDtypeStruct(state.shape,...  21.5 us
    unnamed x12, local copies, waits for them, and re-layouts  3.8 us

profile of v2, /device:TPU:1, one launch (start us, length us, event | category | flops | bytes accessed | tf_op | source)
XLA Modules:
  0.0 94.7 jit_solution(17380621510825487038)
XLA Ops:
  0.0 0.0 copy-start.4
  0.0 1.3 %broadcast_in_dim.6.val_ref = f32[4,1,256]{2,1,0:T(1,128)} reshape(f32[4,256]{1,0:T(4,128)} %param.10) | data formatting | bytes 8192 | tf_op jit(solution)/shard_map/broadcast_in_dim | solution.py:554
  1.3 1.3 %broadcast_in_dim.7.var_ref = f32[4,1,256]{2,1,0:T(1,128)} reshape(f32[4,256]{1,0:T(4,128)} %param.11) | data formatting | bytes 8192 | tf_op jit(solution)/shard_map/broadcast_in_dim | solution.py:554
  2.6 0.7 add_select_fusion.1
  3.3 0.6 pad_add_fusion.obs_ref
  3.9 0.6 pad_add_fusion.1.batch_ref.obs_ref
  4.5 0.0 copy-start.3
  4.5 64.9 %forecast.1 = (f32[16,4,3,32,128]{4,3,2,1,0:T(8,128)}, f32[4,64,256]{2,1,0:T(8,128)}, f32[4,64,256]{2,1,0:T(8,128)}) custom-call(f32[4,3,32,2048]{3,2,1,0:T(8,128)} %ens_ref.1, f32[32,2048]{1,0:T(8,128)} %depth_ref.1, s32[32,128]{1,0:T(8,128)} %cut_ref.3, s32[2,1024]{1,0:T(2,128)} %pad_add_fusion.obs_ref, s32[4,2,256]{2,1,0:T(2,128)} %pad_add_fusion.1.batch_ref.obs_ref, ...), custom_call_target="tpu_custom_call" | custom-call | tf_op jit(solution)/shard_map/forecast/pallas_call | solution.py:353
  69.4 0.0 copy-done.4
  69.4 0.0 copy-done.3
  69.5 0.0 copy-start
  69.5 1.9 %copy-done = f32[16,4,3,32,128]{4,3,2,1,0:T(8,128)S(1)} copy-done((f32[16,4,3,32,128]{4,3,2,1,0:T(8,128)S(1)}, f32[16,4,3,32,128]{4,3,2,1,0:T(8,128)}, u32[]{:S(2)}) %copy-start) | copy-done | bytes 3145752
  71.3 0.0 copy-start.1
  71.3 0.9 %copy-done.1 = f32[4,64,256]{2,1,0:T(8,128)S(1)} copy-done((f32[4,64,256]{2,1,0:T(8,128)S(1)}, f32[4,64,256]{2,1,0:T(8,128)}, u32[]{:S(2)}) %copy-start.1) | copy-done | bytes 262168
  72.3 0.0 copy-start.2
  72.3 0.9 %copy-done.2 = f32[4,64,256]{2,1,0:T(8,128)S(1)} copy-done((f32[4,64,256]{2,1,0:T(8,128)S(1)}, f32[4,64,256]{2,1,0:T(8,128)}, u32[]{:S(2)}) %copy-start.2) | copy-done | bytes 262168
  73.2 21.5 %update.1 = f32[64,3,32,128]{3,2,1,0:T(8,128)} custom-call(f32[64,3,32,128]{3,2,1,0:T(8,128)S(1)} %bitcast.8, f32[4,64,256]{2,1,0:T(8,128)S(1)} %copy-done.1, f32[4,64,256]{2,1,0:T(8,128)S(1)} %copy-done.2, s32[4,2,256]{2,1,0:T(2,128)S(1)} %copy-done.3, s32[32,128]{1,0:T(8,128)S(1)} %copy-done.4), custom_call_target="tpu_custom_call" | custom-call | tf_op jit(solution)/shard_map/update/pallas_call | solution.py:523
  (4 shorter events, 0.0 us)
Async XLA Ops:
  0.0 69.4 %copy-start.4 = (s32[32,128]{1,0:T(8,128)S(1)}, s32[32,128]{1,0:T(8,128)}, u32[]{:S(2)}) copy-start(s32[32,128]{1,0:T(8,128)} %cut_ref.3) | copy-start | bytes 49156
  4.5 64.9 %copy-start.3 = (s32[4,2,256]{2,1,0:T(2,128)S(1)}, s32[4,2,256]{2,1,0:T(2,128)}, u32[]{:S(2)}) copy-start(s32[4,2,256]{2,1,0:T(2,128)} %pad_add_fusion.1.batch_ref.obs_ref) | copy-start | bytes 24580
  69.5 1.9 %copy-start = (f32[16,4,3,32,128]{4,3,2,1,0:T(8,128)S(1)}, f32[16,4,3,32,128]{4,3,2,1,0:T(8,128)}, u32[]{:S(2)}) copy-start(f32[16,4,3,32,128]{4,3,2,1,0:T(8,128)} %get-tuple-element.8) | copy-start | bytes 9437188
  71.3 0.9 %copy-start.1 = (f32[4,64,256]{2,1,0:T(8,128)S(1)}, f32[4,64,256]{2,1,0:T(8,128)}, u32[]{:S(2)}) copy-start(f32[4,64,256]{2,1,0:T(8,128)} %get-tuple-element.9.at_ref) | copy-start | bytes 786436
  72.3 0.9 %copy-start.2 = (f32[4,64,256]{2,1,0:T(8,128)S(1)}, f32[4,64,256]{2,1,0:T(8,128)}, u32[]{:S(2)}) copy-start(f32[4,64,256]{2,1,0:T(8,128)} %get-tuple-element.10.wt_ref) | copy-start | bytes 786436

commit v3 on v2

--- a/solution.py
+++ b/solution.py
@@ -17,6 +17,7 @@
 BF16 = jnp.bfloat16
 HALO = 8
 CHUNK = 32
+GROUP = 8
 LANES = 128
 
 
@@ -35,6 +36,14 @@
 def split2(x):
     hi = x.astype(BF16)
     return hi, (x - hi.astype(F32)).astype(BF16)
+
+
+def quot(x, size):
+    return x >> (size.bit_length() - 1)
+
+
+def rest(x, size):
+    return x & (size - 1)
 
 
 def iota(shape, dim):
@@ -46,11 +55,11 @@
     (0, 1), (0, 3), (1, 0), (3, 0), (1, 1), (3, 3), (1, 3), (3, 1),
     (0, 2), (2, 0), (2, 1), (2, 3), (1, 2), (3, 2), (2, 2),
 )
-EARLY = 15
+EARLY = 2
 
 
 def forecast_kernel(
-    ens_ref, depth_ref, cut_ref, obs_ref, batch_ref, val_ref, var_ref,
+    ens_ref, depth_ref, cut_ref, obs_ref, val_ref, var_ref,
     out_ref, at_ref, wt_ref,
     ext, dep, hbuf, fbuf, gbuf, part, slots, mine, prior_ref, staged, flat, heights, cuts,
     lsem, hs_sem, hr_sem, ds_sem, dr_sem, s1_sem, r1_sem, s2_sem, r2_sem, bs_sem, br_sem, own_sem,
@@ -61,7 +70,7 @@
     sub = lax.axis_index("sub")
     n_mem = lax.axis_size("mem")
     n_sub = lax.axis_size("sub")
-    nobs = obs_ref.shape[1]
+    nobs = obs_ref.shape[0] * obs_ref.shape[1]
 
     barrier = pltpu.get_barrier_semaphore()
     for k in range(1, n_sub):
@@ -101,14 +110,15 @@
         for cp in halo_copies(m):
             cp.start()
 
-    obs_x = obs_ref[0:1, :]
-    obs_y = obs_ref[1:2, :]
+    index = jnp.concatenate([obs_ref[b:b + 1, :] for b in range(obs_ref.shape[0])], 1)
+    obs_x = quot(index, cols)
+    obs_y = rest(index, cols)
     local_x = obs_x - sub * rows
     in_rows = (local_x >= 0) & (local_x < rows)
-    combo = jnp.where(in_rows, (obs_y // LANES) * rows + local_x, -1)
-    lane_of = obs_y % LANES
-
-    in_block = in_rows & (obs_y // LANES == me)
+    combo = jnp.where(in_rows, quot(obs_y, LANES) * rows + local_x, -1)
+    lane_of = rest(obs_y, LANES)
+
+    in_block = in_rows & (quot(obs_y, LANES) == me)
     pick_row = jnp.where(in_block, local_x, -1)
     cut_t = jnp.transpose(cut_ref[...].astype(F32))
     row_hot = jnp.where(iota((rows, nobs), 0) == pick_row, 1.0, 0.0)
@@ -187,9 +197,9 @@
                 staged[t, m, f] = ext[m, f, pl.ds(HALO, rows), cols_of(t)]
         own_copy(m).start()
 
-        @pl.when(m == 0)
+        @pl.when(m < EARLY)
         def _():
-            for cp in block_copies(m, 0, EARLY):
+            for cp in block_copies(m, 0, len(ORDER)):
                 cp.start()
 
         block = 256
@@ -235,19 +245,16 @@
             device_id=(lax.rem(me + k, n_mem), sub), device_id_type=MESH)
         cp.start()
         second.append(cp)
-    for cp in block_copies(0, EARLY, len(ORDER)):
-        cp.start()
-
     def rest_body(m, _):
         for cp in block_copies(m, 0, len(ORDER)):
             cp.start()
         return 0
 
-    lax.fori_loop(1, members, rest_body, 0)
+    lax.fori_loop(EARLY, members, rest_body, 0)
     for cp in second:
         cp.wait()
-    weights(prior_ref, batch_ref, val_ref, var_ref, at_ref, wt_ref, flat, heights, cuts,
-            float(rows * n_sub), float(cols))
+    weights(prior_ref, obs_ref, val_ref, var_ref, at_ref, wt_ref, flat, heights, cuts,
+            rows * n_sub, cols)
 
     def finish_body(m, _):
         for cp in block_copies(m, 0, len(ORDER)):
@@ -282,36 +289,41 @@
         h = heights[b]
         mean = jnp.mean(h, 0, keepdims=True)
         at = h - mean
-        inv_var = 1.0 / var_ref[b]
+        inv_var = 1.0 / var_ref[pl.ds(b, 1), :]
         scaled = at * inv_var
         gram = nt(scaled, at, HIGHEST) * scale
         eye = jnp.where(iota((members, members), 0) == iota((members, members), 1), 1.0, 0.0)
-        aug = jnp.concatenate([gram + eye, eye], 1)
-
-        def eliminate(g, x):
+        x = jnp.concatenate([eye, gram + eye], 1)
+        line = iota(x.shape, 0)
+        for k in range(0, members, 8):
+            ahead = [jnp.broadcast_to(x[:, members + k + l:members + k + l + 1], x.shape) for l in range(8)]
             for j in range(0, 8, 2):
-                col0 = jnp.broadcast_to(x[:, j:j + 1], x.shape)
-                col1 = jnp.broadcast_to(x[:, j + 1:j + 2], x.shape)
-                a, b01, c = col0[j:j + 1], col1[j:j + 1], col1[j + 1:j + 2]
+                p, q = k + j, k + j + 1
+                col0, col1 = ahead[0], ahead[1]
+                a, b01, c = col0[p:p + 1], col1[p:p + 1], col1[q:q + 1]
                 inv = 1.0 / (a * c - b01 * b01)
-                row0 = (c * x[j:j + 1] - b01 * x[j + 1:j + 2]) * inv
-                row1 = (a * x[j + 1:j + 2] - b01 * x[j:j + 1]) * inv
-                fixed = x - col0 * row0 - col1 * row1
-                x = jnp.where(iota(x.shape, 0) == j, row0, jnp.where(iota(x.shape, 0) == j + 1, row1, fixed))
-            x = jnp.concatenate([x[8:], x[:8]], 0)
-            return pltpu.roll(x, x.shape[1] - 8, 1)
-
-        aug = lax.fori_loop(0, members // 8, eliminate, aug)
-        inverse = aug[:, 0:members]
-        big = nn(inverse, scaled, HIGHEST)
-        gap = (val_ref[b] - mean) * inv_var
+                a, b01, c = a * inv, b01 * inv, c * inv
+
+                def sweep(y):
+                    row0 = c * y[p:p + 1] - b01 * y[q:q + 1]
+                    row1 = a * y[q:q + 1] - b01 * y[p:p + 1]
+                    left = y - col0 * row0 - col1 * row1
+                    return jnp.where(line == p, row0, jnp.where(line == q, row1, left))
+
+                ahead = [sweep(y) for y in ahead[2:]]
+                x = sweep(x)
+        inverse = x[:, 0:members]
+        big = nn3(inverse, scaled)
+        gap = (val_ref[pl.ds(b, 1), :] - mean) * inv_var
         lean = jnp.sum(at * gap, 1, keepdims=True)
         small = gap - scale * jnp.sum(big * lean, 0, keepdims=True)
         wt = small - 0.5 * big
         at_ref[b] = at * scale
         wt_ref[b] = wt
 
-        xy = jnp.concatenate([jnp.broadcast_to(obs_ref[b, k:k + 1, :].astype(F32), (4, nobs)) for k in range(2)], 0)
+        here = obs_ref[pl.ds(b, 1), :]
+        xy = jnp.concatenate(
+            [jnp.broadcast_to(k.astype(F32), (4, nobs)) for k in (quot(here, size_y), rest(here, size_y))], 0)
         xy = jnp.transpose(xy)
         from_x = xy[:, 0:1]
         from_y = xy[:, 4:5]
@@ -322,9 +334,10 @@
             hc = heights[c]
             dev_hi, dev_lo = split2(hc - jnp.mean(hc, 0, keepdims=True))
             cross = nn(anom_hi, dev_hi) + (nn(anom_hi, dev_lo) + nn(anom_lo, dev_hi))
-            gx = jnp.abs(obs_ref[c, 0:1, :].astype(F32) - from_x)
+            there = obs_ref[pl.ds(c, 1), :]
+            gx = jnp.abs(quot(there, size_y).astype(F32) - from_x)
             gx = jnp.minimum(gx, size_x - gx)
-            gy = jnp.abs(obs_ref[c, 1:2, :].astype(F32) - from_y)
+            gy = jnp.abs(rest(there, size_y).astype(F32) - from_y)
             gy = jnp.minimum(gy, size_y - gy)
             near = jnp.maximum(1.0 - (gx * gx + gy * gy) * cuts[c], 0.0)
             gain_hi, gain_lo = split2(cross * (near * near))
@@ -337,12 +350,12 @@
     lax.fori_loop(0, batches, batch_body, 0)
 
 
-def forecast(ensemble, sea_depth, cutoff, obs_xy, obs, values, variance):
+def forecast(ensemble, sea_depth, cutoff, obs, values, variance):
     per, fields, rows, cols = ensemble.shape
     n_mem = lax.axis_size("mem")
     n_sub = lax.axis_size("sub")
     members = per * n_mem
-    batches, _, nobs = obs.shape
+    batches, nobs = obs.shape
     total = batches * nobs
     tiles = cols // LANES
     width = per * 8 + total // LANES
@@ -357,7 +370,7 @@
             jax.ShapeDtypeStruct((batches, members, nobs), F32),
             jax.ShapeDtypeStruct((batches, members, nobs), F32),
         ),
-        in_specs=[hbm, hbm] + [vmem] * 5,
+        in_specs=[hbm, hbm] + [vmem] * 4,
         out_specs=(hbm, vmem, vmem),
         scratch_shapes=[
             vm((per, fields, rows + 2 * HALO, cols), F32),
@@ -380,19 +393,22 @@
         compiler_params=pltpu.CompilerParams(
             collective_id=0, has_side_effects=True, vmem_limit_bytes=56 << 20),
         name="forecast",
-    )(ensemble, sea_depth, cutoff, obs_xy, obs, values, variance)
-
-
-def update_kernel(state_ref, at_ref, wt_ref, obs_ref, cut_ref, out_ref,
-                  lhs1, lhs2, far_x, sq_y, inv_r2, work, rhs1, begin, stage, counts, in_sems, sems):
+    )(ensemble, sea_depth, cutoff, obs, values, variance)
+
+
+def update_kernel(state_ref, at_hbm, wt_hbm, obs_ref, cut_ref, out_ref,
+                  at_ref, wt_ref, lhs1, lhs2, far_x, sq_y, inv_r2, work, begin, stage, counts, in_sems, sems, w_sems):
     members, fields, rows, _ = state_ref.shape
     batches, _, nobs = at_ref.shape
-    block = work.shape[1] // (fields * LANES)
+    block = work.shape[2] // (fields * LANES)
     size_x = rows * lax.axis_size("sub")
     size_y = LANES * lax.axis_size("mem")
     x0 = lax.axis_index("sub") * rows
     y0 = lax.axis_index("mem") * LANES
 
+    early = [pltpu.make_async_copy(at_hbm, at_ref, w_sems.at[0]), pltpu.make_async_copy(wt_hbm, wt_ref, w_sems.at[1])]
+    for cp in early:
+        cp.start()
     for step in range(rows // block):
         pltpu.make_async_copy(
             state_ref.at[:, :, pl.ds(step * block, block)], begin.at[step], in_sems.at[step]).start()
@@ -411,8 +427,8 @@
         return jnp.where(inside, 0, jnp.minimum(before, after))
 
     def select(b, _):
-        ox = obs_ref[b, 0:1, :]
-        oy = obs_ref[b, 1:2, :]
+        ox = quot(obs_ref[pl.ds(b, 1), :], size_y)
+        oy = rest(obs_ref[pl.ds(b, 1), :], size_y)
         gx = gap_to(ox, x0, rows, size_x)
         gy = gap_to(oy, y0, LANES, size_y)
         keep = jnp.where(gx * gx + gy * gy < reach, 1.0, 0.0)
@@ -447,6 +463,8 @@
         lax.fori_loop(0, chunks, pack, 0)
         return 0
 
+    for cp in early:
+        cp.wait()
     lax.fori_loop(0, batches, select, 0)
 
     slabs = fields * block
@@ -469,24 +487,20 @@
         source = begin.at[step].reshape(members * slabs, LANES)
         target = stage.at[step].reshape(members * slabs, LANES)
         for s in range(slabs):
-            work[:, s * LANES:(s + 1) * LANES] = source[place(s), :]
-
-        def batch_body(b, _):
-            for s in range(slabs):
-                span = slice(s * LANES, (s + 1) * LANES)
-                hi, lo = split2(work[:, span])
-                rhs1[0:members, span] = hi
-                rhs1[members:2 * members, span] = lo
-                rhs1[2 * members:, span] = hi
+            work[0, :, s * LANES:(s + 1) * LANES] = source[place(s), :]
+
+        def batch_body(b, now):
+            chunks = counts[b]
 
             def chunk_body(c, _):
                 left = lhs1[b, c]
                 right = lhs2[b, c]
                 px = far_x[b, c]
                 dy = sq_y[b, c]
-                for r in range(0, block, 2):
+                base = jnp.where(c == 0, now, 1 - now)
+                for r in range(0, block, GROUP):
                     near = []
-                    for k in (r, r + 1):
+                    for k in range(r, r + GROUP):
                         row = step * block + k
                         gx = jnp.abs(px - (x0 + row).astype(F32))
                         gx = jnp.minimum(gx, size_x - gx)
@@ -494,17 +508,18 @@
                         part = jnp.maximum(1.0 - ratio, 0.0)
                         near += [part * part] * fields
                     near = jnp.concatenate(near, 1)
-                    span = slice(r * fields * LANES, (r + 2) * fields * LANES)
-                    hi, lo = split2(nn(left, rhs1[:, span]) * near)
-                    work[:, span] += nn(right, jnp.concatenate([hi, lo, hi], 0))
+                    span = slice(r * fields * LANES, (r + GROUP) * fields * LANES)
+                    hi, lo = split2(work[now, :, span])
+                    hi, lo = split2(nn(left, jnp.concatenate([hi, lo, hi], 0)) * near)
+                    work[1 - now, :, span] = work[base, :, span] + nn(right, jnp.concatenate([hi, lo, hi], 0))
                 return 0
 
-            lax.fori_loop(0, counts[b], chunk_body, 0)
-            return 0
-
-        lax.fori_loop(0, batches, batch_body, 0)
+            lax.fori_loop(0, chunks, chunk_body, 0)
+            return jnp.where(chunks > 0, 1 - now, now)
+
+        last = lax.fori_loop(0, batches, batch_body, 0)
         for s in range(slabs):
-            target[place(s), :] = work[:, s * LANES:(s + 1) * LANES]
+            target[place(s), :] = work[last, :, s * LANES:(s + 1) * LANES]
         out_copy(step).start()
         return 0
 
@@ -523,23 +538,25 @@
     return pl.pallas_call(
         update_kernel,
         out_shape=jax.ShapeDtypeStruct(state.shape, F32),
-        in_specs=[pl.BlockSpec(memory_space=pl.ANY)] + [vmem] * 4,
+        in_specs=[pl.BlockSpec(memory_space=pl.ANY)] * 3 + [vmem] * 2,
         out_specs=pl.BlockSpec(memory_space=pl.ANY),
         scratch_shapes=[
+            pltpu.VMEM(at.shape, F32),
+            pltpu.VMEM(wt.shape, F32),
             pltpu.VMEM((batches, chunks, CHUNK, 3 * members), BF16),
             pltpu.VMEM((batches, chunks, members, 3 * CHUNK), BF16),
             pltpu.VMEM((batches, chunks, CHUNK, LANES), F32),
             pltpu.VMEM((batches, chunks, CHUNK, LANES), F32),
             pltpu.VMEM((rows, LANES), F32),
-            pltpu.VMEM((members, width), F32),
-            pltpu.VMEM((3 * members, width), BF16),
+            pltpu.VMEM((2, members, width), F32),
             pltpu.VMEM((rows // block, members, fields, block, LANES), F32),
             pltpu.VMEM((rows // block, members, fields, block, LANES), F32),
             pltpu.SMEM((batches,), jnp.int32),
             pltpu.SemaphoreType.DMA((rows // block,)),
             pltpu.SemaphoreType.DMA((rows // block,)),
+            pltpu.SemaphoreType.DMA((2,)),
         ],
-        compiler_params=pltpu.CompilerParams(vmem_limit_bytes=40 << 20),
+        compiler_params=pltpu.CompilerParams(vmem_limit_bytes=63 << 20),
         name="update",
     )(state, at, wt, obs, cutoff)
 
@@ -547,12 +564,8 @@
 def local(ensemble, sea_depth, cutoff, obs_index, obs_value, obs_var):
     per, fields, rows, cols = ensemble.shape
     members = per * lax.axis_size("mem")
-    obs_x = obs_index // cols
-    obs_y = obs_index % cols
-    obs = jnp.stack([obs_x, obs_y], 1)
-    flat = jnp.stack([obs_x.reshape(-1), obs_y.reshape(-1)], 0)
-    state, at, wt = forecast(ensemble, sea_depth, cutoff, flat, obs, obs_value[:, None, :], obs_var[:, None, :])
-    return update(state.reshape(members, fields, rows, LANES), at, wt, obs, cutoff)
+    state, at, wt = forecast(ensemble, sea_depth, cutoff, obs_index, obs_value, obs_var)
+    return update(state.reshape(members, fields, rows, LANES), at, wt, obs_index, cutoff)
 
 
 def solution(mesh):

time: 95.2 us -> 74.6 us (0.78)
  Pallas kernels: 86.4 us -> 74.1 us
  local copies, waits for them, and re-layouts: 6.38 us -> 0 us
  other arithmetic: 1.91 us -> 0 us
    pallas_call x1, Pallas kernels: 64.9 us -> 58.7 us  [forecast(): pl.pallas_call(forecast_kernel, out_shape=(jax.ShapeDtypeStruct((n_mem, p...]
    pallas_call x1, Pallas kernels: 21.5 us -> 15.4 us  [update(): pl.pallas_call(update_kernel, out_shape=jax.ShapeDtypeStruct(state.shape,...]
    unnamed x12 -> x0, local copies, waits for them, and re-layouts: 3.8 us -> none
    broadcast_in_dim x2 -> x0, local copies, waits for them, and re-layouts: 2.57 us -> none  [the longest x1 1.3 us: local(): obs_value[:, None, :]]
    another operation x2 -> x0, other arithmetic: 1.21 us -> none  [the longest x1 0.61 us: local(): flat = jnp.stack([obs_x.reshape(-1), obs_y.reshape(-1)], 0)]
where the time goes in v3:
time: 74.6 us; the launch traced here: 74.1 us
  Pallas kernels  74.1 us (99%)
    pallas_call x1, Pallas kernels, forecast(): pl.pallas_call(forecast_kernel, out_shape=(jax.ShapeDtypeStruct((n_mem, p...  58.7 us
    pallas_call x1, Pallas kernels, update(): pl.pallas_call(update_kernel, out_shape=jax.ShapeDtypeStruct(state.shape,...  15.4 us

profile of v3, /device:TPU:1, one launch (start us, length us, event | category | flops | bytes accessed | tf_op | source)
XLA Modules:
  0.0 74.1 jit_solution(8394822356069984860)
XLA Ops:
  0.0 58.7 %forecast.1 = (f32[16,4,3,32,128]{4,3,2,1,0:T(8,128)}, f32[4,64,256]{2,1,0:T(8,128)}, f32[4,64,256]{2,1,0:T(8,128)}) custom-call(f32[4,3,32,2048]{3,2,1,0:T(8,128)} %ens_ref.1, f32[32,2048]{1,0:T(8,128)} %depth_ref.1, s32[32,128]{1,0:T(8,128)} %cut_ref.3, s32[4,256]{1,0:T(4,128)} %obs_ref.3, f32[4,256]{1,0:T(4,128)} %val_ref.1, f32[4,256]{1,0:T(4,128)} %var_ref.1), custom_call_target="tpu_custom_call" | custom-call | tf_op jit(solution)/shard_map/forecast/pallas_call | solution.py:366
  58.8 15.4 %update.1 = f32[64,3,32,128]{3,2,1,0:T(8,128)} custom-call(f32[64,3,32,128]{3,2,1,0:T(8,128)} %bitcast.1, f32[4,64,256]{2,1,0:T(8,128)} %get-tuple-element.9.at_hbm, f32[4,64,256]{2,1,0:T(8,128)} %get-tuple-element.10.wt_hbm, s32[4,256]{1,0:T(4,128)} %obs_ref.3, s32[32,128]{1,0:T(8,128)} %cut_ref.3), custom_call_target="tpu_custom_call" | custom-call | tf_op jit(solution)/shard_map/update/pallas_call | solution.py:538

commit v4 on v3

--- a/solution.py
+++ b/solution.py
@@ -56,6 +56,7 @@
     (0, 2), (2, 0), (2, 1), (2, 3), (1, 2), (3, 2), (2, 2),
 )
 EARLY = 2
+SOME = 5
 
 
 def forecast_kernel(
@@ -125,7 +126,29 @@
     cut_cols = nn(cut_t.astype(BF16), row_hot.astype(BF16))
     cut_obs = jnp.sum(jnp.where(iota((LANES, nobs), 0) == lane_of, cut_cols, 0.0), 0, keepdims=True)
     for q in range(nobs // LANES):
-        mine[pl.ds(members * 8 + q, 1), :] = cut_obs[:, q * LANES:(q + 1) * LANES]
+        mine[0, q:q + 1, :] = cut_obs[:, q * LANES:(q + 1) * LANES]
+
+    def send_part(s):
+        part[sub, s] = mine[s]
+        for k in range(1, n_sub):
+            pltpu.make_async_remote_copy(
+                mine.at[s], part.at[sub, s], s1_sem.at[s], r1_sem.at[s],
+                device_id=(me, lax.rem(sub + k, n_sub)), device_id_type=MESH).start()
+
+    def send_total(s):
+        all_parts = part.at[pl.ds(0, n_sub - 1), s]
+        pltpu.make_async_copy(all_parts, all_parts, r1_sem.at[s]).wait()
+        total = part[0, s]
+        for k in range(1, n_sub):
+            total = total + part[k, s]
+        slots[s] = total
+        prior_ref[me, s] = total
+        for k in range(1, n_mem):
+            pltpu.make_async_remote_copy(
+                slots.at[s], prior_ref.at[me, s], s2_sem.at[s], r2_sem.at[s],
+                device_id=(lax.rem(me + k, n_mem), sub), device_id_type=MESH).start()
+
+    send_part(0)
 
     halo[0].wait()
     halo[1].wait()
@@ -143,7 +166,7 @@
     def cols_of(t):
         return pl.ds(t * LANES, LANES)
 
-    def spread(load):
+    def spread(load, lane):
         first_east = pltpu.roll(load(0), LANES - 1, 1)
         east = first_east
         west_before = pltpu.roll(load(tiles - 1), 1, 1)
@@ -160,7 +183,7 @@
         for n, (dz, dx) in list(enumerate(ORDER))[first:last]:
             peer = lax.rem(me // SIDE + dz, SIDE) * SIDE + lax.rem(lax.rem(me, SIDE) + dx, SIDE)
             found.append(pltpu.make_async_remote_copy(
-                staged.at[peer, m], out_ref.at[me, m], bs_sem.at[n, m], br_sem.at[n, m],
+                staged.at[peer, m], out_ref.at[me, m], bs_sem.at[m], br_sem.at[m],
                 device_id=(peer, sub), device_id_type=MESH))
         return found
 
@@ -175,7 +198,7 @@
             hbuf[t, here] = ext[m, 0, :, cols_of(t)]
 
         def step_body(s, carry):
-            for t, h_dy in spread(lambda t: hbuf[t, here]):
+            for t, h_dy in spread(lambda t: hbuf[t, here], lane):
                 u = ext[m, 1, :, cols_of(t)]
                 v = ext[m, 2, :, cols_of(t)]
                 u1 = u + ((DT * CORIOLIS) * v - half * (hbuf[t, above] - hbuf[t, below]))
@@ -185,16 +208,26 @@
                 ext[m, 2, :, cols_of(t)] = v1
                 fbuf[t, here] = d * u1
                 gbuf[t] = d * v1
-            for t, g_dy in spread(lambda t: gbuf[t]):
+            for t, g_dy in spread(lambda t: gbuf[t], lane):
                 hbuf[t, here] = hbuf[t, here] - half * (fbuf[t, above] - fbuf[t, below] + g_dy)
             return carry
 
-        lax.fori_loop(0, STEPS, step_body, 0)
+        lax.fori_loop(0, STEPS - 1, step_body, 0)
         inner = pl.ds(2 * HALO, rows)
-        for t in range(tiles):
-            staged[t, m, 0] = hbuf[t, inner]
-            for f in range(1, fields):
-                staged[t, m, f] = ext[m, f, pl.ds(HALO, rows), cols_of(t)]
+        north, south = pl.ds(2 * HALO + 1, rows), pl.ds(2 * HALO - 1, rows)
+        own = pl.ds(HALO, rows)
+        for t, h_dy in spread(lambda t: hbuf[t, inner], lane[:rows]):
+            u = ext[m, 1, :, cols_of(t)]
+            v = ext[m, 2, :, cols_of(t)]
+            u1 = u + ((DT * CORIOLIS) * v - half * (hbuf[t, above] - hbuf[t, below]))
+            v1 = v[HALO:HALO + rows] - ((DT * CORIOLIS) * u[HALO:HALO + rows] + half * h_dy)
+            d = dep[:, cols_of(t)]
+            staged[t, m, 1] = u1[HALO:HALO + rows]
+            staged[t, m, 2] = v1
+            fbuf[t, here] = d * u1
+            gbuf[t, own] = d[HALO:HALO + rows] * v1
+        for t, g_dy in spread(lambda t: gbuf[t, own], lane[:rows]):
+            staged[t, m, 0] = hbuf[t, inner] - half * (fbuf[t, north] - fbuf[t, south] + g_dy)
         own_copy(m).start()
 
         @pl.when(m < EARLY)
@@ -202,63 +235,55 @@
             for cp in block_copies(m, 0, len(ORDER)):
                 cp.start()
 
+        @pl.when(m == EARLY)
+        def _():
+            for cp in block_copies(m, 0, SOME):
+                cp.start()
+
+        send_total(m)
         block = 256
         turned = jnp.concatenate(
-            [jnp.transpose(jnp.concatenate([hbuf[t, inner] for t in range(4 * g, 4 * g + 4)], 0))
+            [jnp.transpose(jnp.concatenate([staged[t, m, 0] for t in range(4 * g, 4 * g + 4)], 0))
              for g in range(tiles // 4)], 1)
-        hi = turned.astype(BF16)
-        rest = turned - hi.astype(F32)
-        mid = rest.astype(BF16)
-        low = (rest - mid.astype(F32)).astype(BF16)
-        parts = jnp.concatenate([hi, mid, low], 0)
+        parts = jnp.concatenate(split2(turned), 0)
         for q in range(nobs // block):
             span = slice(q * block, (q + 1) * block)
             hot = jnp.where(iota((tiles * rows, block), 0) == combo[:, span], 1.0, 0.0).astype(BF16)
             picked = nn(parts, hot)
-            picked = picked[0:LANES] + picked[LANES:2 * LANES] + picked[2 * LANES:]
+            picked = picked[0:LANES] + picked[LANES:]
             got = jnp.sum(jnp.where(iota((LANES, block), 0) == lane_of[:, span], picked, 0.0), 0, keepdims=True)
             for s in range(block // LANES):
-                mine[pl.ds(m * 8 + q * (block // LANES) + s, 1), :] = got[:, s * LANES:(s + 1) * LANES]
+                mine[m + 1, pl.ds(q * (block // LANES) + s, 1), :] = got[:, s * LANES:(s + 1) * LANES]
+        send_part(m + 1)
         return 0
 
     lax.fori_loop(0, members, member_body, 0)
 
-    part[sub] = mine[...]
-    first = []
-    for k in range(1, n_sub):
-        cp = pltpu.make_async_remote_copy(
-            mine, part.at[sub], s1_sem.at[k], r1_sem.at[k],
-            device_id=(me, lax.rem(sub + k, n_sub)), device_id_type=MESH)
+    send_total(members)
+
+    for cp in block_copies(EARLY, SOME, len(ORDER)):
         cp.start()
-        first.append(cp)
-    for cp in first:
-        cp.wait()
-    total = part[0]
-    for k in range(1, n_sub):
-        total = total + part[k]
-    slots[...] = total
-    prior_ref[me] = total
-    second = []
-    for k in range(1, n_mem):
-        cp = pltpu.make_async_remote_copy(
-            slots, prior_ref.at[me], s2_sem.at[k], r2_sem.at[k],
-            device_id=(lax.rem(me + k, n_mem), sub), device_id_type=MESH)
-        cp.start()
-        second.append(cp)
+
     def rest_body(m, _):
         for cp in block_copies(m, 0, len(ORDER)):
             cp.start()
         return 0
 
-    lax.fori_loop(EARLY, members, rest_body, 0)
-    for cp in second:
-        cp.wait()
+    lax.fori_loop(EARLY + 1, members, rest_body, 0)
+    def totals_body(s, _):
+        for sent, sems, count in ((part, s1_sem, n_sub), (prior_ref, s2_sem, n_mem), (prior_ref, r2_sem, n_mem)):
+            peers = sent.at[pl.ds(0, count - 1), s]
+            pltpu.make_async_copy(peers, peers, sems.at[s]).wait()
+        return 0
+
+    lax.fori_loop(0, members + 1, totals_body, 0)
     weights(prior_ref, obs_ref, val_ref, var_ref, at_ref, wt_ref, flat, heights, cuts,
             rows * n_sub, cols)
 
     def finish_body(m, _):
-        for cp in block_copies(m, 0, len(ORDER)):
-            cp.wait()
+        peers = out_ref.at[pl.ds(0, n_mem - 1), m]
+        for sems in (bs_sem, br_sem):
+            pltpu.make_async_copy(peers, peers, sems.at[m]).wait()
         own_copy(m).wait()
         return 0
 
@@ -272,12 +297,11 @@
 
 
 def weights(prior_ref, obs_ref, val_ref, var_ref, at_ref, wt_ref, flat, heights, cuts, size_x, size_y):
-    n_mem, width, _ = prior_ref.shape
+    n_mem, width, _, _ = prior_ref.shape
     batches, members, nobs = at_ref.shape
-    per = members // n_mem
     groups = batches * nobs // LANES
-    flat[...] = prior_ref[:, 0:per * 8, :].reshape(members * 8, LANES)
-    cut = jnp.sum(prior_ref[:, per * 8:per * 8 + groups, :], 0)
+    flat[...] = prior_ref[:, 1:].reshape(members * 8, LANES)
+    cut = jnp.sum(prior_ref[:, 0], 0)
     cut = 1.0 / (cut * cut)
     for q in range(groups):
         b, s = q * LANES // nobs, q * LANES % nobs
@@ -358,7 +382,7 @@
     batches, nobs = obs.shape
     total = batches * nobs
     tiles = cols // LANES
-    width = per * 8 + total // LANES
+    slot = (per + 1, total // LANES, LANES)
     vmem = pl.BlockSpec(memory_space=pltpu.VMEM)
     hbm = pl.BlockSpec(memory_space=pl.ANY)
     dma = pltpu.SemaphoreType.DMA
@@ -378,17 +402,17 @@
             vm((tiles, rows + 4 * HALO, LANES), F32),
             vm((tiles, rows + 4 * HALO, LANES), F32),
             vm((tiles, rows + 2 * HALO, LANES), F32),
-            vm((n_sub, width, LANES), F32),
-            vm((width, LANES), F32),
-            vm((width, LANES), F32),
-            vm((n_mem, width, LANES), F32),
+            vm((n_sub, *slot), F32),
+            vm(slot, F32),
+            vm(slot, F32),
+            vm((n_mem, *slot), F32),
             vm((tiles, per, fields, rows, LANES), F32),
             vm((members * 8, LANES), F32),
             vm((batches, members, nobs), F32),
             vm((batches, 1, nobs), F32),
             dma((per + 1,)), dma((2, per)), dma((2, per)), dma((2,)), dma((2,)),
-            dma((n_sub,)), dma((n_sub,)), dma((n_mem,)), dma((n_mem,)),
-            dma((n_mem, per)), dma((n_mem, per)), dma((per,)),
+            dma((per + 1,)), dma((per + 1,)), dma((per + 1,)), dma((per + 1,)),
+            dma((per,)), dma((per,)), dma((per,)),
         ],
         compiler_params=pltpu.CompilerParams(
             collective_id=0, has_side_effects=True, vmem_limit_bytes=56 << 20),

time: 74.6 us -> 73.7 us (0.988)
  no operation moved by 1% of the time
where the time goes in v4:
time: 73.7 us; the launch traced here: 73.4 us
  Pallas kernels  73.4 us (100%)
    pallas_call x1, Pallas kernels, forecast(): pl.pallas_call(forecast_kernel, out_shape=(jax.ShapeDtypeStruct((n_mem, p...  58 us
    pallas_call x1, Pallas kernels, update(): pl.pallas_call(update_kernel, out_shape=jax.ShapeDtypeStruct(state.shape,...  15.4 us

profile of v4, /device:TPU:1, one launch (start us, length us, event | category | flops | bytes accessed | tf_op | source)
XLA Modules:
  0.0 73.4 jit_solution(8799432787313234022)
XLA Ops:
  0.0 58.0 %forecast.1 = (f32[16,4,3,32,128]{4,3,2,1,0:T(8,128)}, f32[4,64,256]{2,1,0:T(8,128)}, f32[4,64,256]{2,1,0:T(8,128)}) custom-call(f32[4,3,32,2048]{3,2,1,0:T(8,128)} %ens_ref.1, f32[32,2048]{1,0:T(8,128)} %depth_ref.1, s32[32,128]{1,0:T(8,128)} %cut_ref.3, s32[4,256]{1,0:T(4,128)} %obs_ref.3, f32[4,256]{1,0:T(4,128)} %val_ref.1, f32[4,256]{1,0:T(4,128)} %var_ref.1), custom_call_target="tpu_custom_call" | custom-call | tf_op jit(solution)/shard_map/forecast/pallas_call | solution.py:390
  58.1 15.4 %update.1 = f32[64,3,32,128]{3,2,1,0:T(8,128)} custom-call(f32[64,3,32,128]{3,2,1,0:T(8,128)} %bitcast.1, f32[4,64,256]{2,1,0:T(8,128)} %get-tuple-element.9.at_hbm, f32[4,64,256]{2,1,0:T(8,128)} %get-tuple-element.10.wt_hbm, s32[4,256]{1,0:T(4,128)} %obs_ref.3, s32[32,128]{1,0:T(8,128)} %cut_ref.3), custom_call_target="tpu_custom_call" | custom-call | tf_op jit(solution)/shard_map/update/pallas_call | solution.py:562

commit v5 on v4

--- a/solution.py
+++ b/solution.py
@@ -16,7 +16,7 @@
 F32 = jnp.float32
 BF16 = jnp.bfloat16
 HALO = 8
-CHUNK = 32
+CHUNK = 40
 GROUP = 8
 LANES = 128
 
@@ -472,9 +472,9 @@
             hot = jnp.where(rank == want, 1.0, 0.0)
             hot16 = hot.astype(BF16)
             lhs1[b, c] = nt(hot16, a3).astype(BF16)
-            zero = jnp.zeros_like(hot16)
+            zero = jnp.zeros_like(hot)
             turn = jnp.concatenate(
-                [jnp.concatenate([hot16, hot16, zero], 0), jnp.concatenate([zero, zero, hot16], 0)], 1)
+                [jnp.concatenate([hot, hot, zero], 0), jnp.concatenate([zero, zero, hot], 0)], 1).astype(BF16)
             lhs2[b, c] = nt(w2, turn).astype(BF16)
             px = jnp.sum(hot * ox.astype(F32), 1, keepdims=True)
             py = jnp.sum(hot * oy.astype(F32), 1, keepdims=True)
@@ -534,8 +534,10 @@
                     near = jnp.concatenate(near, 1)
                     span = slice(r * fields * LANES, (r + GROUP) * fields * LANES)
                     hi, lo = split2(work[now, :, span])
-                    hi, lo = split2(nn(left, jnp.concatenate([hi, lo, hi], 0)) * near)
-                    work[1 - now, :, span] = work[base, :, span] + nn(right, jnp.concatenate([hi, lo, hi], 0))
+                    gain = nn(left, jnp.concatenate([hi, lo, hi], 0)) * near
+                    top = gain.astype(BF16).astype(F32)
+                    stacked = jnp.concatenate([top, gain - top, top], 0).astype(BF16)
+                    work[1 - now, :, span] = work[base, :, span] + nn(right, stacked)
                 return 0
 
             lax.fori_loop(0, chunks, chunk_body, 0)
@@ -556,7 +558,7 @@
     members, fields, rows, _ = state.shape
     batches, _, nobs = at.shape
     block = 8
-    chunks = nobs // CHUNK
+    chunks = pl.cdiv(nobs, CHUNK)
     vmem = pl.BlockSpec(memory_space=pltpu.VMEM)
     width = fields * block * LANES
     return pl.pallas_call(

time: 73.7 us -> 73.7 us (level)
  no operation moved by 1% of the time
where the time goes in v5:
time: 73.7 us; the launch traced here: 73.5 us
  Pallas kernels  73.5 us (100%)
    pallas_call x1, Pallas kernels, forecast(): pl.pallas_call(forecast_kernel, out_shape=(jax.ShapeDtypeStruct((n_mem, p...  58 us
    pallas_call x1, Pallas kernels, update(): pl.pallas_call(update_kernel, out_shape=jax.ShapeDtypeStruct(state.shape,...  15.4 us

profile of v5, /device:TPU:1, one launch (start us, length us, event | category | flops | bytes accessed | tf_op | source)
XLA Modules:
  0.0 73.5 jit_solution(6312219512757341944)
XLA Ops:
  0.0 58.0 %forecast.1 = (f32[16,4,3,32,128]{4,3,2,1,0:T(8,128)}, f32[4,64,256]{2,1,0:T(8,128)}, f32[4,64,256]{2,1,0:T(8,128)}) custom-call(f32[4,3,32,2048]{3,2,1,0:T(8,128)} %ens_ref.1, f32[32,2048]{1,0:T(8,128)} %depth_ref.1, s32[32,128]{1,0:T(8,128)} %cut_ref.3, s32[4,256]{1,0:T(4,128)} %obs_ref.3, f32[4,256]{1,0:T(4,128)} %val_ref.1, f32[4,256]{1,0:T(4,128)} %var_ref.1), custom_call_target="tpu_custom_call" | custom-call | tf_op jit(solution)/shard_map/forecast/pallas_call | solution.py:390
  58.1 15.4 %update.1 = f32[64,3,32,128]{3,2,1,0:T(8,128)} custom-call(f32[64,3,32,128]{3,2,1,0:T(8,128)} %bitcast.1, f32[4,64,256]{2,1,0:T(8,128)} %get-tuple-element.9.at_hbm, f32[4,64,256]{2,1,0:T(8,128)} %get-tuple-element.10.wt_hbm, s32[4,256]{1,0:T(4,128)} %obs_ref.3, s32[32,128]{1,0:T(8,128)} %cut_ref.3), custom_call_target="tpu_custom_call" | custom-call | tf_op jit(solution)/shard_map/update/pallas_call | solution.py:564

commit v6 on v5

--- a/solution.py
+++ b/solution.py
@@ -56,7 +56,7 @@
     (0, 2), (2, 0), (2, 1), (2, 3), (1, 2), (3, 2), (2, 2),
 )
 EARLY = 2
-SOME = 5
+SOME = 8
 
 
 def forecast_kernel(

time: 73.7 us -> 73.7 us (level); the launches traced: 73.5 us -> 72.7 us
  Pallas kernels: 73.5 us -> 72.7 us
    pallas_call x1, Pallas kernels: 58 us -> 57.2 us  [forecast(): pl.pallas_call(forecast_kernel, out_shape=(jax.ShapeDtypeStruct((n_mem, p...]
where the time goes in v6:
time: 73.7 us; the launch traced here: 72.7 us
  Pallas kernels  72.7 us (99%)
    pallas_call x1, Pallas kernels, forecast(): pl.pallas_call(forecast_kernel, out_shape=(jax.ShapeDtypeStruct((n_mem, p...  57.2 us
    pallas_call x1, Pallas kernels, update(): pl.pallas_call(update_kernel, out_shape=jax.ShapeDtypeStruct(state.shape,...  15.4 us

profile of v6, /device:TPU:1, one launch (start us, length us, event | category | flops | bytes accessed | tf_op | source)
XLA Modules:
  0.0 72.7 jit_solution(14363609348441949860)
XLA Ops:
  0.0 57.2 %forecast.1 = (f32[16,4,3,32,128]{4,3,2,1,0:T(8,128)}, f32[4,64,256]{2,1,0:T(8,128)}, f32[4,64,256]{2,1,0:T(8,128)}) custom-call(f32[4,3,32,2048]{3,2,1,0:T(8,128)} %ens_ref.1, f32[32,2048]{1,0:T(8,128)} %depth_ref.1, s32[32,128]{1,0:T(8,128)} %cut_ref.3, s32[4,256]{1,0:T(4,128)} %obs_ref.3, f32[4,256]{1,0:T(4,128)} %val_ref.1, f32[4,256]{1,0:T(4,128)} %var_ref.1), custom_call_target="tpu_custom_call" | custom-call | tf_op jit(solution)/shard_map/forecast/pallas_call | solution.py:390
  57.2 15.4 %update.1 = f32[64,3,32,128]{3,2,1,0:T(8,128)} custom-call(f32[64,3,32,128]{3,2,1,0:T(8,128)} %bitcast.1, f32[4,64,256]{2,1,0:T(8,128)} %get-tuple-element.9.at_hbm, f32[4,64,256]{2,1,0:T(8,128)} %get-tuple-element.10.wt_hbm, s32[4,256]{1,0:T(4,128)} %obs_ref.3, s32[32,128]{1,0:T(8,128)} %cut_ref.3), custom_call_target="tpu_custom_call" | custom-call | tf_op jit(solution)/shard_map/update/pallas_call | solution.py:564
